TPU v7x, 128 devices: a whole 4x4x4 slice. The times are simulated.
128 devices in a mesh: orb: 32 (over z, x, core), grp: 4 (over y).
Axes of the slice: x: 4, y: 4, z: 4, core: 2. Of those that a mesh axis runs over, the one named last changes fastest.
Arguments:
- orbitals: float32 [1024, 32, 1024], P('orb', 'grp'), may hold values from -6 to 6
- anchors: int32 [1024], replicated, may hold values from 0 to 8
- wanted: int32 [32, 32, 1], replicated, may hold values from -1 to 1023, as said below
- pairs: int32 [32, 4, 240, 2], P('orb'), may hold values from 0 to 1023, as said below
- counts: int32 [32, 4], P('orb'), may hold values from 1 to 240, as said below
Outputs:
- exchange_field: float32 [1024, 32, 1024], P('orb', 'grp')
Inputs may be any that keep to these rules, and one draw needn't show every extreme that they name: wanted[r, o] lists up to 1 different orbitals owned by group o (ids o * 32 to o * 32 + 31), -1 in empty slots; wanted[r, r] is empty; in every draw some pairs (r, o) fill all 1 slots. pairs[r, g, p] = (i, c) with i owned by group r and c below 64; a code below 32 never names i itself; pairs may repeat. `counts`: in each group r, one device g holds exactly 240 live pairs.
All inputs are finite; a program needn't handle non-finite values.
Results may differ from a plain program's by a relative error of at most 0.0085.
Values may be sent and summed in bfloat16 or wider, within the bound.
No kernel may reach another device: no remote copies, remote signals or barrier semaphores. Data moves between devices by JAX's collectives and lax.ppermute only.
A program may use at most 128 MiB of HBM per device.

v0:
```python
import math

import jax
import jax.numpy as jnp
from jax import lax
from jax.sharding import PartitionSpec as P

screening = 0.01
block_pairs = 64


def sine_table(extent):
    ordinal = jnp.arange(extent, dtype=jnp.float32) + 1.0
    angles = math.pi * ordinal[:, None] * ordinal[None, :] / (extent + 1)
    return (math.sqrt(2.0 / (extent + 1)) * jnp.sin(angles)).astype(jnp.bfloat16)


def denominator(extent):
    ordinal = jnp.arange(extent, dtype=jnp.float32) + 1.0
    eigenvalue = 4.0 * jnp.sin(math.pi * ordinal / (2 * (extent + 1))) ** 2
    return (
        eigenvalue[:, None, None]
        + eigenvalue[None, :, None]
        + eigenvalue[None, None, :]
        + screening
    )


def selector(offset, extent, dtype):
    target_row = jnp.arange(extent, dtype=jnp.int32)[None, :, None]
    source_row = jnp.arange(extent, dtype=jnp.int32)[None, None, :]
    return (source_row == target_row - offset[:, None, None]).astype(dtype)


def potential(density, sine_rows, blocks, divisor):
    batch_size, extent, plane_size = density.shape

    def along_first(values):
        return jnp.einsum("kx,pxq->pkq", sine_rows, values, preferred_element_type=jnp.float32)

    def along_last(values):
        flat_rows = values.reshape(batch_size * extent * plane_size // 128, 128)
        product = jnp.dot(flat_rows, blocks, preferred_element_type=jnp.float32)
        return product.reshape(batch_size, extent, plane_size)

    def along_middle(values):
        cube = values.reshape(batch_size, extent, extent, extent)
        product = jnp.einsum("ky,pxyz->pxkz", sine_rows, cube, preferred_element_type=jnp.float32)
        return product.reshape(batch_size, extent, plane_size)

    section_one = along_first(density).astype(jnp.bfloat16)
    section_two = along_last(section_one).astype(jnp.bfloat16)
    section_three = (along_middle(section_two) / divisor).astype(jnp.bfloat16)
    section_four = along_middle(section_three).astype(jnp.bfloat16)
    section_five = along_last(section_four).astype(jnp.bfloat16)
    return along_first(section_five).astype(jnp.bfloat16)


def pair_terms(first_boxes, second_boxes, offset, sine_rows, blocks, divisor):
    extent = first_boxes.shape[1]
    forward = selector(offset, extent, jnp.bfloat16)
    shifted_box = jnp.einsum(
        "pxa,paq->pxq", forward, second_boxes, preferred_element_type=jnp.float32
    ).astype(jnp.bfloat16)
    density = (first_boxes.astype(jnp.float32) * shifted_box.astype(jnp.float32)).astype(
        jnp.bfloat16
    )
    field_wide = potential(density, sine_rows, blocks, divisor).astype(jnp.float32)
    own_term = field_wide * shifted_box.astype(jnp.float32)
    backward = selector(-offset, extent, jnp.float32)
    other_term = jnp.einsum(
        "pxa,paq->pxq",
        backward,
        field_wide * first_boxes.astype(jnp.float32),
        precision=lax.Precision.HIGHEST,
    )
    return (own_term, other_term)


def shards(orbitals, anchors, wanted, pairs, counts):
    group_size = lax.axis_size("grp")
    member = lax.axis_index("orb")
    position = lax.axis_index("grp")
    own_count = orbitals.shape[0]
    extent = orbitals.shape[1] * group_size
    plane_size = orbitals.shape[2]
    sine_rows = sine_table(extent)
    blocks = jnp.kron(jnp.eye(128 // extent, dtype=jnp.bfloat16), sine_rows)
    divisor = denominator(extent).reshape(extent, plane_size)
    slab_boxes = orbitals.astype(jnp.bfloat16)
    own_full = lax.all_gather(slab_boxes, "grp", axis=1, tiled=True)
    owner_rows = wanted.shape[0]
    per_owner = wanted.shape[2]
    slot_count = owner_rows * per_owner
    send_ids = lax.dynamic_index_in_dim(wanted, member, 1, keepdims=False).reshape(slot_count)
    send_live = send_ids >= 0
    send_local = jnp.where(send_live, send_ids - member * own_count, 0)
    outgoing = jnp.where(
        send_live[:, None, None], own_full[send_local], jnp.zeros((), jnp.bfloat16)
    )
    partner_full = lax.all_to_all(outgoing, "orb", split_axis=0, concat_axis=0, tiled=True)
    group_pairs = pairs[0]
    group_counts = counts[0]
    listed = lax.dynamic_index_in_dim(group_pairs, position, 0, keepdims=False)
    live_total = lax.dynamic_index_in_dim(group_counts, position, 0, keepdims=False)
    listed = jnp.concatenate([listed, jnp.zeros((block_pairs, 2), jnp.int32)], axis=0)
    first_ids = listed[:, 0]
    codes = listed[:, 1]
    request_rows = lax.dynamic_index_in_dim(wanted, member, 0, keepdims=False).reshape(slot_count)
    first_local = jnp.clip(first_ids - member * own_count, 0, own_count - 1)
    second_own = codes < own_count
    second_local = jnp.clip(codes, 0, own_count - 1)
    second_slot = jnp.clip(codes - own_count, 0, slot_count - 1)
    far_ids = request_rows[second_slot]
    second_ids = jnp.where(second_own, member * own_count + second_local, far_ids)
    valid = second_ids >= 0
    offsets = anchors[jnp.maximum(second_ids, 0)] - anchors[first_ids]

    def turn(turn_index, running):
        own_sum, partner_sum = running
        start_row = turn_index * block_pairs

        def window(values):
            return lax.dynamic_slice_in_dim(values, start_row, block_pairs, 0)

        in_range = (start_row + jnp.arange(block_pairs, dtype=jnp.int32) < live_total) & window(
            valid
        )
        from_own = window(second_own)
        first_boxes = own_full[window(first_local)]
        second_boxes = jnp.where(
            from_own[:, None, None],
            own_full[window(second_local)],
            partner_full[window(second_slot)],
        )
        own_term, other_term = pair_terms(
            first_boxes, second_boxes, window(offsets), sine_rows, blocks, divisor
        )
        own_sum = own_sum.at[jnp.where(in_range, window(first_local), own_count)].add(
            own_term, mode="drop"
        )
        own_sum = own_sum.at[jnp.where(in_range & from_own, window(second_local), own_count)].add(
            other_term, mode="drop"
        )
        partner_sum = partner_sum.at[
            jnp.where(in_range & ~from_own, window(second_slot), slot_count)
        ].add(other_term, mode="drop")
        return (own_sum, partner_sum)

    rounds = (live_total + block_pairs - 1) // block_pairs
    own_acc = jnp.zeros((own_count, extent, plane_size), jnp.float32)
    partner_acc = jnp.zeros((slot_count, extent, plane_size), jnp.float32)
    own_acc, partner_acc = lax.fori_loop(0, rounds, turn, (own_acc, partner_acc))
    returned = lax.all_to_all(
        partner_acc.astype(jnp.bfloat16), "orb", split_axis=0, concat_axis=0, tiled=True
    ).astype(partner_acc.dtype)
    own_acc = own_acc.at[jnp.where(send_live, send_local, own_count)].add(returned, mode="drop")
    result = lax.psum_scatter(
        own_acc.astype(jnp.bfloat16), "grp", scatter_dimension=1, tiled=True
    ).astype(jnp.float32)
    return result


def solution(mesh):
    return jax.shard_map(
        shards,
        mesh=mesh,
        in_specs=(P("orb", "grp", None), P(), P(), P("orb", None, None, None), P("orb", None)),
        out_specs=P("orb", "grp", None),
        check_vma=False,
    )
```

profile of v0, /device:TPU:1, one launch (start us, length us, event | category | flops | bytes accessed | tf_op | source)
XLA Modules:
  0.0 1087.3 jit_solution(4677255508980015248)
XLA Ops:
  14.1 28.7 %all-gather.2.cloned.1.call-done = bf16[32,32,1024]{2,1,0:T(8,128)(2,1)} async-done(((bf16[32,8,1024]{2,1,0:T(8,128)(2,1)}), bf16[32,32,1024]{2,1,0:T(8,128)(2,1)}) %all-gather.2.cloned.1.call-update) | async-done | bytes 2097168 | tf_op jit(solution)/shard_map/all_gather | solution.py:91
  89.4 910.9 %while.14 = (s32[]{:T(128)}, f32[32,32,1024]{2,1,0:T(8,128)}, f32[32,32,1024]{2,1,0:T(8,128)}, s32[]{:T(128)}, s32[]{:T(128)}, /*index=5*/pred[304]{0:T(512)(128...) while((s32[]{:T(128)}, f32[32,32,1024]{2,1,0:T(8,128)}, ...), condition=%wide.region_4.5_spmd.clone.clone, body=%wide.region_0.4_spmd.clone.clone.sunk | while | flops 2596512512 | bytes 256338384 | solution.py:153
  127.3 18.7 %convert_element_type.230 = bf16[64,32,32,32]{3,2,1,0:T(8,128)(2,1)} reshape(bf16[16384,128]{1,0:T(8,128)(2,1)} %convolution_convert_fusion.5) | data formatting | bytes 8388608 | tf_op jit(solution)/shard_map/while/body/convert_element_type | solution.py:52
  146.0 27.1 %copy.20 = bf16[64,32,32,32]{0,2,3,1:T(8,128)(2,1)} copy(bf16[64,32,32,32]{3,2,1,0:T(8,128)(2,1)} %convert_element_type.230) | data formatting | bytes 8388608 | tf_op jit(solution)/shard_map/while/body/convert_element_type | solution.py:52
  183.1 29.3 %copy.21 = bf16[64,32,32,32]{3,2,1,0:T(8,128)(2,1)} copy(bf16[64,32,32,32]{0,2,3,1:T(8,128)(2,1)} %convert_bitcast_fusion.6) | data formatting | bytes 8388608 | tf_op jit(solution)/shard_map/while/body/convert_element_type | solution.py:54
  212.3 19.6 %convert_element_type.231 = bf16[16384,128]{1,0:T(8,128)(2,1)} reshape(bf16[64,32,32,32]{3,2,1,0:T(8,128)(2,1)} %copy.21) | data formatting | bytes 8388608 | tf_op jit(solution)/shard_map/while/body/convert_element_type | solution.py:54
  260.1 19.3 %scatter_fusion.2 = f32[32,32,1024]{2,1,0:T(8,128)} fusion(f32[32,32,1024]{2,1,0:T(8,128)} %get-tuple-element.483, s32[64]{0:T(128)S(1)} %get-tuple-element.457, f32[64,32,1024]{2,1,0:T(8,128)} %fusion.93), kind=kCustom, calls=%fused_computation.8.clone.clone.1 | custom fusion | flops 2097152 | bytes 25166080 | tf_op jit(solution)/shard_map/while/body/scatter-add | solution.py:147
  279.5 19.1 %scatter_fusion = f32[32,32,1024]{2,1,0:T(8,128)} fusion(f32[32,32,1024]{2,1,0:T(8,128)} %get-tuple-element.482, s32[64]{0:T(128)S(1)} %get-tuple-element.448, f32[64,32,1024]{2,1,0:T(8,128)} %get-tuple-element.453), kind=kCustom, calls=%fused_computation.6.clone.clone.1 | custom fusion | flops 2097152 | bytes 25166080 | tf_op jit(solution)/shard_map/while/body/scatter-add | solution.py:139
  298.6 18.4 %scatter_fusion.1 = f32[32,32,1024]{2,1,0:T(8,128)} fusion(f32[32,32,1024]{2,1,0:T(8,128)} %scatter_fusion, s32[64]{0:T(128)S(1)} %get-tuple-element.454, f32[64,32,1024]{2,1,0:T(8,128)} %fusion.93), kind=kCustom, calls=%fused_computation.7.clone.clone.1 | custom fusion | flops 2097152 | bytes 25166080 | tf_op jit(solution)/shard_map/while/body/scatter-add | solution.py:142
  354.9 18.7 %convert_element_type.230 = bf16[64,32,32,32]{3,2,1,0:T(8,128)(2,1)} reshape(bf16[16384,128]{1,0:T(8,128)(2,1)} %convolution_convert_fusion.5) | data formatting | bytes 8388608 | tf_op jit(solution)/shard_map/while/body/convert_element_type | solution.py:52
  373.7 27.1 %copy.20 = bf16[64,32,32,32]{0,2,3,1:T(8,128)(2,1)} copy(bf16[64,32,32,32]{3,2,1,0:T(8,128)(2,1)} %convert_element_type.230) | data formatting | bytes 8388608 | tf_op jit(solution)/shard_map/while/body/convert_element_type | solution.py:52
  410.7 29.3 %copy.21 = bf16[64,32,32,32]{3,2,1,0:T(8,128)(2,1)} copy(bf16[64,32,32,32]{0,2,3,1:T(8,128)(2,1)} %convert_bitcast_fusion.6) | data formatting | bytes 8388608 | tf_op jit(solution)/shard_map/while/body/convert_element_type | solution.py:54
  439.9 19.6 %convert_element_type.231 = bf16[16384,128]{1,0:T(8,128)(2,1)} reshape(bf16[64,32,32,32]{3,2,1,0:T(8,128)(2,1)} %copy.21) | data formatting | bytes 8388608 | tf_op jit(solution)/shard_map/while/body/convert_element_type | solution.py:54
  487.8 19.3 %scatter_fusion.2 = f32[32,32,1024]{2,1,0:T(8,128)} fusion(f32[32,32,1024]{2,1,0:T(8,128)} %get-tuple-element.483, s32[64]{0:T(128)S(1)} %get-tuple-element.457, f32[64,32,1024]{2,1,0:T(8,128)} %fusion.93), kind=kCustom, calls=%fused_computation.8.clone.clone.1 | custom fusion | flops 2097152 | bytes 25166080 | tf_op jit(solution)/shard_map/while/body/scatter-add | solution.py:147
  507.1 19.3 %scatter_fusion = f32[32,32,1024]{2,1,0:T(8,128)} fusion(f32[32,32,1024]{2,1,0:T(8,128)} %get-tuple-element.482, s32[64]{0:T(128)S(1)} %get-tuple-element.448, f32[64,32,1024]{2,1,0:T(8,128)} %get-tuple-element.453), kind=kCustom, calls=%fused_computation.6.clone.clone.1 | custom fusion | flops 2097152 | bytes 25166080 | tf_op jit(solution)/shard_map/while/body/scatter-add | solution.py:139
  526.3 18.6 %scatter_fusion.1 = f32[32,32,1024]{2,1,0:T(8,128)} fusion(f32[32,32,1024]{2,1,0:T(8,128)} %scatter_fusion, s32[64]{0:T(128)S(1)} %get-tuple-element.454, f32[64,32,1024]{2,1,0:T(8,128)} %fusion.93), kind=kCustom, calls=%fused_computation.7.clone.clone.1 | custom fusion | flops 2097152 | bytes 25166080 | tf_op jit(solution)/shard_map/while/body/scatter-add | solution.py:142
  582.8 18.7 %convert_element_type.230 = bf16[64,32,32,32]{3,2,1,0:T(8,128)(2,1)} reshape(bf16[16384,128]{1,0:T(8,128)(2,1)} %convolution_convert_fusion.5) | data formatting | bytes 8388608 | tf_op jit(solution)/shard_map/while/body/convert_element_type | solution.py:52
  601.5 27.1 %copy.20 = bf16[64,32,32,32]{0,2,3,1:T(8,128)(2,1)} copy(bf16[64,32,32,32]{3,2,1,0:T(8,128)(2,1)} %convert_element_type.230) | data formatting | bytes 8388608 | tf_op jit(solution)/shard_map/while/body/convert_element_type | solution.py:52
  638.5 29.3 %copy.21 = bf16[64,32,32,32]{3,2,1,0:T(8,128)(2,1)} copy(bf16[64,32,32,32]{0,2,3,1:T(8,128)(2,1)} %convert_bitcast_fusion.6) | data formatting | bytes 8388608 | tf_op jit(solution)/shard_map/while/body/convert_element_type | solution.py:54
  667.8 19.6 %convert_element_type.231 = bf16[16384,128]{1,0:T(8,128)(2,1)} reshape(bf16[64,32,32,32]{3,2,1,0:T(8,128)(2,1)} %copy.21) | data formatting | bytes 8388608 | tf_op jit(solution)/shard_map/while/body/convert_element_type | solution.py:54
  715.6 19.2 %scatter_fusion.2 = f32[32,32,1024]{2,1,0:T(8,128)} fusion(f32[32,32,1024]{2,1,0:T(8,128)} %get-tuple-element.483, s32[64]{0:T(128)S(1)} %get-tuple-element.457, f32[64,32,1024]{2,1,0:T(8,128)} %fusion.93), kind=kCustom, calls=%fused_computation.8.clone.clone.1 | custom fusion | flops 2097152 | bytes 25166080 | tf_op jit(solution)/shard_map/while/body/scatter-add | solution.py:147
  734.8 19.3 %scatter_fusion = f32[32,32,1024]{2,1,0:T(8,128)} fusion(f32[32,32,1024]{2,1,0:T(8,128)} %get-tuple-element.482, s32[64]{0:T(128)S(1)} %get-tuple-element.448, f32[64,32,1024]{2,1,0:T(8,128)} %get-tuple-element.453), kind=kCustom, calls=%fused_computation.6.clone.clone.1 | custom fusion | flops 2097152 | bytes 25166080 | tf_op jit(solution)/shard_map/while/body/scatter-add | solution.py:139
  754.1 18.4 %scatter_fusion.1 = f32[32,32,1024]{2,1,0:T(8,128)} fusion(f32[32,32,1024]{2,1,0:T(8,128)} %scatter_fusion, s32[64]{0:T(128)S(1)} %get-tuple-element.454, f32[64,32,1024]{2,1,0:T(8,128)} %fusion.93), kind=kCustom, calls=%fused_computation.7.clone.clone.1 | custom fusion | flops 2097152 | bytes 25166080 | tf_op jit(solution)/shard_map/while/body/scatter-add | solution.py:142
  810.4 18.7 %convert_element_type.230 = bf16[64,32,32,32]{3,2,1,0:T(8,128)(2,1)} reshape(bf16[16384,128]{1,0:T(8,128)(2,1)} %convolution_convert_fusion.5) | data formatting | bytes 8388608 | tf_op jit(solution)/shard_map/while/body/convert_element_type | solution.py:52
  829.1 27.1 %copy.20 = bf16[64,32,32,32]{0,2,3,1:T(8,128)(2,1)} copy(bf16[64,32,32,32]{3,2,1,0:T(8,128)(2,1)} %convert_element_type.230) | data formatting | bytes 8388608 | tf_op jit(solution)/shard_map/while/body/convert_element_type | solution.py:52
  866.1 29.3 %copy.21 = bf16[64,32,32,32]{3,2,1,0:T(8,128)(2,1)} copy(bf16[64,32,32,32]{0,2,3,1:T(8,128)(2,1)} %convert_bitcast_fusion.6) | data formatting | bytes 8388608 | tf_op jit(solution)/shard_map/while/body/convert_element_type | solution.py:54
  895.4 19.6 %convert_element_type.231 = bf16[16384,128]{1,0:T(8,128)(2,1)} reshape(bf16[64,32,32,32]{3,2,1,0:T(8,128)(2,1)} %copy.21) | data formatting | bytes 8388608 | tf_op jit(solution)/shard_map/while/body/convert_element_type | solution.py:54
  943.2 19.9 %scatter_fusion.2 = f32[32,32,1024]{2,1,0:T(8,128)} fusion(f32[32,32,1024]{2,1,0:T(8,128)} %get-tuple-element.483, s32[64]{0:T(128)S(1)} %get-tuple-element.457, f32[64,32,1024]{2,1,0:T(8,128)} %fusion.93), kind=kCustom, calls=%fused_computation.8.clone.clone.1 | custom fusion | flops 2097152 | bytes 25166080 | tf_op jit(solution)/shard_map/while/body/scatter-add | solution.py:147
  963.1 18.7 %scatter_fusion = f32[32,32,1024]{2,1,0:T(8,128)} fusion(f32[32,32,1024]{2,1,0:T(8,128)} %get-tuple-element.482, s32[64]{0:T(128)S(1)} %get-tuple-element.448, f32[64,32,1024]{2,1,0:T(8,128)} %get-tuple-element.453), kind=kCustom, calls=%fused_computation.6.clone.clone.1 | custom fusion | flops 2097152 | bytes 25166080 | tf_op jit(solution)/shard_map/while/body/scatter-add | solution.py:139
  981.8 18.3 %scatter_fusion.1 = f32[32,32,1024]{2,1,0:T(8,128)} fusion(f32[32,32,1024]{2,1,0:T(8,128)} %scatter_fusion, s32[64]{0:T(128)S(1)} %get-tuple-element.454, f32[64,32,1024]{2,1,0:T(8,128)} %fusion.93), kind=kCustom, calls=%fused_computation.7.clone.clone.1 | custom fusion | flops 2097152 | bytes 25166080 | tf_op jit(solution)/shard_map/while/body/scatter-add | solution.py:142
  1002.9 31.1 %all_to_all.10 = bf16[32,32,1024]{2,1,0:T(8,128)(2,1)S(1)} all-to-all(bf16[32,32,1024]{2,1,0:T(8,128)(2,1)S(1)} %convert_element_type.103), channel_id=1, replica_groups=mesh['orb'=32,'grp'=4] {'orb'}, dimensions={0} | all-to-all | bytes 4194304 | tf_op jit(solution)/shard_map/all_to_all | solution.py:154
  1050.1 27.7 %reduce-scatter.4.cloned.1.call-done = bf16[8,32768]{1,0:T(8,128)(2,1)} async-done(((bf16[32,32768]{1,0:T(8,128)(2,1)}), bf16[8,32768]{1,0:T(8,128)(2,1)}) %reduce-scatter.4.cloned.1.call-update) | async-done | bytes 524304
  (166 shorter events, 378.3 us)
Async XLA Ops:
  6.5 48.7 %copy-start = (s32[1,4,240,2]{2,3,1,0:T(2,128)S(1)}, s32[1,4,240,2]{2,3,1,0:T(2,128)}, u32[]{:S(2)}) copy-start(s32[1,4,240,2]{2,3,1,0:T(2,128)} %param.10) | copy-start | bytes 23044
  6.5 36.3 %all-gather.2.cloned.1.call-start = ((), (), s32[]{:S(2)}) async-start(), calls=%async_computation.3 | async-start | bytes 2621440 | tf_op jit(solution)/shard_map/all_gather | solution.py:91
  45.1 31.7 %copy-start.2 = (s32[1024]{0:T(1024)S(1)}, s32[1024]{0:T(1024)}, u32[]{:S(2)}) copy-start(s32[1024]{0:T(1024)} %param.8) | copy-start | bytes 12292
  46.7 36.4 %all-to-all-start = ((bf16[32,32,1024]{2,1,0:T(8,128)(2,1)}), bf16[32,32,1024]{2,1,0:T(8,128)(2,1)S(1)}, u32[]{:S(2)}, u32[]{:S(2)}) async-start(bf16[32,32,1024]{2,1,0:T(8,128)(2,1)} %broadcast_select_fusion), calls=%async_computation | async-start | bytes 4194304 | tf_op jit(solution)/shard_map/all_to_all | solution.py:101
  54.5 1023.3 %reduce-scatter.4.cloned.1.call-start = ((), (), s32[]{:S(2)}) async-start(), calls=%async_computation.4 | async-start | bytes 2621440
  83.1 1.3 copy-start.5
  84.4 5.0 copy-start.4
  89.4 0.5 copy-start.6
  146.0 27.1 %copy-start.7 = (f32[32]{0:T(128)S(1)}, f32[32]{0:T(128)}, u32[]{:S(2)}) copy-start(f32[32]{0:T(128)} %copy-done.6) | copy-start | bytes 388 | tf_op jit(solution)/shard_map/while
  244.7 8.3 copy-start.3
  317.0 0.5 copy-start.6
  373.7 27.1 %copy-start.7 = (f32[32]{0:T(128)S(1)}, f32[32]{0:T(128)}, u32[]{:S(2)}) copy-start(f32[32]{0:T(128)} %copy-done.6) | copy-start | bytes 388 | tf_op jit(solution)/shard_map/while
  472.4 8.3 copy-start.3
  544.9 0.5 copy-start.6
  601.5 27.1 %copy-start.7 = (f32[32]{0:T(128)S(1)}, f32[32]{0:T(128)}, u32[]{:S(2)}) copy-start(f32[32]{0:T(128)} %copy-done.6) | copy-start | bytes 388 | tf_op jit(solution)/shard_map/while
  700.2 8.3 copy-start.3
  772.5 0.5 copy-start.6
  829.1 27.1 %copy-start.7 = (f32[32]{0:T(128)S(1)}, f32[32]{0:T(128)}, u32[]{:S(2)}) copy-start(f32[32]{0:T(128)} %copy-done.6) | copy-start | bytes 388 | tf_op jit(solution)/shard_map/while
  927.8 8.3 copy-start.3
  1034.0 2.5 copy-start.8
  1046.0 34.5 %copy-start.1 = (s32[1,4,240,2]{2,3,1,0:T(2,128)S(1)}, s32[1,4,240,2]{2,3,1,0:T(2,128)}, u32[]{:S(2)}) copy-start(s32[1,4,240,2]{2,3,1,0:T(2,128)} %param.10) | copy-start | bytes 23044
Sparse Core Ops, SparseCore 0:
  9.0 33.8 all-gather.1
  1050.2 27.5 reduce-scatter.3
where the time goes:
time: 1090 us
  local copies, waits for them, and re-layouts  498 us (46%)
  other arithmetic  279 us (26%)
  matrix products  198 us (18%)
  waiting for transfers between devices  59 us (5%)
  blocking collectives  31.1 us (3%)
  between operations  14.2 us (1%)
    convert_element_type x8, local copies, waits for them, and re-layouts, potential(): section_four = along_middle(section_three).astype(jnp.bfloat16)  196 us
    convert_element_type x8, local copies, waits for them, and re-layouts, potential(): section_two = along_last(section_one).astype(jnp.bfloat16)  183 us
    scatter-add x4, other arithmetic, turn(): partner_sum = partner_sum.at[jnp.where(in_range & ~from_own, window(secon...  77.8 us
    scatter-add x4, other arithmetic, turn(): own_sum.at[jnp.where(in_range, window(first_local), own_count)]  76.3 us
    scatter-add x4, other arithmetic, turn(): own_sum.at[jnp.where(in_range & from_own, window(second_local), own_count)]  73.7 us
    dot_general x8, matrix products, along_first(): jnp.einsum('kx,pxq->pkq', sine_rows, values, preferred_element_type=jnp.f...  60.3 us
    dot_general x8, matrix products, along_last(): product = jnp.dot(flat_rows, blocks, preferred_element_type=jnp.float32)  43.4 us
    dot_general x4, matrix products, along_middle(): jnp.einsum('ky,pxyz->pxkz', sine_rows, cube, preferred_element_type=jnp.f...  39.1 us
  transfers between devices with their start and end apart: 3, of which 3 were waited for; matrix products, arithmetic and copies ran while one was open for 3% of the time, Pallas kernels for 0%

commit v1 on v0

v1 whole, which is shorter than its diff:
```python
import math

import jax
import jax.numpy as jnp
import numpy as np
from jax import lax
from jax.experimental import pallas as pl
from jax.experimental.pallas import tpu as pltpu
from jax.sharding import PartitionSpec as P

screening = 0.01
EXT = 32
HALF = EXT // 2
PLANE = EXT * EXT
CHUNKS = PLANE // 128
MARGIN = 8
PAD = EXT + 2 * MARGIN
BATCH = 8
LIST = 256
F32 = jnp.float32
BF16 = jnp.bfloat16


def tables():
    ordinal = np.arange(EXT, dtype=np.float64) + 1.0
    sine = math.sqrt(2.0 / (EXT + 1)) * np.sin(math.pi * ordinal[:, None] * ordinal[None, :] / (EXT + 1))
    sine = sine.astype(np.float32).astype(jnp.bfloat16).astype(np.float64)
    eigen = 4.0 * np.sin(math.pi * ordinal / (2 * (EXT + 1))) ** 2
    blocks, inverse = [], []
    for y_odd in (0, 1):
        for z_odd in (0, 1):
            blocks.append(np.kron(sine[:HALF, y_odd::2], sine[:HALF, z_odd::2]))
            plane = (eigen[y_odd::2, None] + eigen[None, z_odd::2]).reshape(-1)
            inverse.append(1.0 / (eigen[:, None] + plane[None, :] + screening))
    return (
        np.stack(blocks).astype(jnp.bfloat16),
        np.kron(np.eye(BATCH), sine).astype(jnp.bfloat16),
        np.stack(inverse).astype(np.float32),
    )


def source_of(position):
    quadrant = position >> 8
    y = (position >> 4) & 15
    z = position & 15
    y = jnp.where((quadrant & 2) != 0, EXT - 1 - y, y)
    z = jnp.where((quadrant & 1) != 0, EXT - 1 - z, z)
    return y * EXT + z


def order_kernel(wanted, orbitals, slab, outgoing, matrix, ordered):
    member = lax.axis_index("orb")
    for c in range(CHUNKS):
        source = source_of(lax.broadcasted_iota(jnp.int32, (PLANE, 128), 1) + c * 128)
        row = lax.broadcasted_iota(jnp.int32, (PLANE, 128), 0)
        matrix[:, c * 128 : (c + 1) * 128] = (row == source).astype(F32).astype(BF16)
    ordered[...] = jnp.dot(orbitals[...].astype(BF16), matrix[...], preferred_element_type=F32)
    slab[...] = ordered[...].astype(BF16)

    def local(r):
        return jnp.clip(wanted[r, member] - member * 32, 0, 31)

    for r in range(0, 32, 2):
        low = ordered[pl.ds(pl.multiple_of(local(r) * 8, 8), 8), :]
        high = ordered[pl.ds(pl.multiple_of(local(r + 1) * 8, 8), 8), :]
        outgoing[r * 8 : r * 8 + 16, :] = jnp.concatenate([low, high], axis=0).astype(BF16)


def list_kernel(pairs, counts, wanted, anchors, own_list, far_list, totals, table):
    member = lax.axis_index("orb")
    position = lax.axis_index("grp")

    def clear(k, carry):
        for u in range(16):
            table[k * 16 + u] = 0
        return carry

    lax.fori_loop(0, 32 * 64 // 16, clear, 0)

    def blank(k, carry):
        for u in range(8):
            own_list[k * 8 + u] = MARGIN << 11
            far_list[k * 8 + u] = MARGIN << 11
        return carry

    lax.fori_loop(0, LIST // 8, blank, 0)
    for g in range(4):

        def note(p, carry):
            cell = (pairs[g, p * 2] & 31) * 64 + pairs[g, p * 2 + 1]
            table[cell] = table[cell] + 1
            return carry

        lax.fori_loop(0, counts[0, g], note, 0)

    def collect(first, target):
        def one(k, found):
            i = k >> 5
            c = (k & 31) + first
            weight = table[i * 64 + c]
            if first:
                other = wanted[member, c - 32]
            else:
                other = member * 32 + c
            live = (weight > 0) & (other >= 0)

            @pl.when(live & ((found & 3) == position))
            def _():
                d = anchors[jnp.maximum(other, 0)] - anchors[member * 32 + i]
                target[found >> 2] = i | (c << 5) | ((d + MARGIN) << 11) | (weight << 16)

            return found + live.astype(jnp.int32)

        found = lax.fori_loop(0, 32 * 32, one, 0)
        return (found - position + 3) >> 2

    totals[0] = collect(0, own_list)
    totals[1] = collect(32, far_list)


def unpack_slab(block, rows, boxes, base, member_of):
    start = pl.multiple_of(MARGIN + 8 * member_of, 8)

    def one(k, carry):
        for c in range(CHUNKS):
            part = block[pl.ds(k * 16, 16), c * 128 : (c + 1) * 128].astype(F32)
            boxes[pl.ds(base + 2 * k, 2), c, pl.ds(start, 8), :] = part.reshape(2, 8, 128)
        return carry

    lax.fori_loop(0, rows // 16, one, 0)


def fill(refs, boxes, base):
    position = lax.axis_index("grp")
    own, left, right, far_low, far_high = refs
    unpack_slab(own, 256, boxes, base, position)
    unpack_slab(left, 256, boxes, base, (position + 3) & 3)
    unpack_slab(right, 256, boxes, base, (position + 1) & 3)
    unpack_slab(far_low, 128, boxes, base, (position + 2) & 3)
    unpack_slab(far_high, 128, boxes, base + 16, (position + 2) & 3)


def run_pairs(count, listed, boxes, sums, blocks, along_x, inverse, density, field):
    def fields(entry):
        return (entry & 31, (entry >> 5) & 63, MARGIN + MARGIN - ((entry >> 11) & 31), entry >> 16)

    def batch(b, carry):
        for p in range(BATCH):
            i, j, shifted, weight = fields(listed[b * BATCH + p])
            for h in range(2):
                f = []
                for q in range(4):
                    c = 2 * q + h
                    f.append(boxes[i, c, pl.ds(MARGIN, EXT), :] * boxes[j, c, pl.ds(shifted, EXT), :])
                a, bb, cc, d = f
                s1, s2, s3, s4 = a + bb, a - bb, cc + d, cc - d
                for q, v in enumerate((s1 + s3, s2 + s4, s1 - s3, s2 - s4)):
                    density[q, p * EXT : (p + 1) * EXT, h * 128 : (h + 1) * 128] = v.astype(BF16)
        for q in range(4):
            t = jnp.dot(density[q], blocks[q], preferred_element_type=F32).astype(BF16)
            t = jnp.dot(along_x[...], t, preferred_element_type=F32)
            t = (t.reshape(BATCH, EXT, 256) * inverse[q][None]).reshape(BATCH * EXT, 256).astype(BF16)
            t = jnp.dot(along_x[...], t, preferred_element_type=F32).astype(BF16)
            field[q] = lax.dot_general(t, blocks[q], (((1,), (1,)), ((), ())), preferred_element_type=F32)
        for p in range(BATCH):
            i, j, shifted, weight = fields(listed[b * BATCH + p])
            scale = weight.astype(F32)
            for h in range(2):
                ee, eo, oe, oo = (
                    field[q, p * EXT : (p + 1) * EXT, h * 128 : (h + 1) * 128] for q in range(4)
                )
                s1, s2, s3, s4 = ee + eo, ee - eo, oe + oo, oe - oo
                for q, v in enumerate((s1 + s3, s2 + s4, s1 - s3, s2 - s4)):
                    c = 2 * q + h
                    v = v * scale
                    sums[i, c, pl.ds(MARGIN, EXT), :] += v * boxes[j, c, pl.ds(shifted, EXT), :]
                    sums[j, c, pl.ds(shifted, EXT), :] += v * boxes[i, c, pl.ds(MARGIN, EXT), :]
        return carry

    lax.fori_loop(0, (count + BATCH - 1) // BATCH, batch, 0)


def clear_rows(ref, first, last):
    def one(k, carry):
        ref[pl.ds(first + k, 1)] = jnp.zeros((1,) + ref.shape[1:], F32)
        return carry

    lax.fori_loop(0, last - first, one, 0)


def own_kernel(totals, listed, s, r, l, r2, l2, blocks, along_x, inverse, out, boxes, sums, density, field):
    clear_rows(boxes, 0, 32)
    clear_rows(sums, 0, 32)
    fill((s, r, l, r2, l2), boxes, 0)
    run_pairs(totals[0], listed, boxes, sums, blocks, along_x, inverse, density, field)

    def one(k, carry):
        for c in range(CHUNKS):
            out[pl.ds(k, 1), c] = sums[pl.ds(k, 1), c, MARGIN : MARGIN + EXT, :]
        return carry

    lax.fori_loop(0, 32, one, 0)


def pack_sums(sums, base, outs):
    position = lax.axis_index("grp")
    for step in range(4):
        start = pl.multiple_of(MARGIN + 8 * ((position + step) & 3), 8)

        def one(k, carry):
            for c in range(CHUNKS):
                part = sums[pl.ds(base + 2 * k, 2), c, pl.ds(start, 8), :].reshape(16, 128)
                outs[step][pl.ds(k * 16, 16), c * 128 : (c + 1) * 128] = part.astype(BF16)
            return carry

        lax.fori_loop(0, 16, one, 0)


def far_kernel(
    totals, listed, before,
    s, r, l, r2, l2,
    fs, fr, fl, fr2, fl2,
    blocks, along_x, inverse,
    o0, o1, o2, o3, f0, f1, f2, f3,
    boxes, sums, density, field,
):
    clear_rows(boxes, 0, 64)
    clear_rows(sums, 32, 64)
    fill((s, r, l, r2, l2), boxes, 0)
    fill((fs, fr, fl, fr2, fl2), boxes, 32)

    def one(k, carry):
        for c in range(CHUNKS):
            sums[pl.ds(k, 1), c, MARGIN : MARGIN + EXT, :] = before[pl.ds(k, 1), c]
        return carry

    lax.fori_loop(0, 32, one, 0)
    run_pairs(totals[1], listed, boxes, sums, blocks, along_x, inverse, density, field)
    pack_sums(sums, 0, (o0, o1, o2, o3))
    pack_sums(sums, 32, (f0, f1, f2, f3))


def finish_kernel(wanted, p0, p1, p2, p3, returned, out, matrix, total):
    member = lax.axis_index("orb")
    for c in range(CHUNKS):
        source = source_of(lax.broadcasted_iota(jnp.int32, (PLANE, 128), 0))
        column = lax.broadcasted_iota(jnp.int32, (PLANE, 128), 1) + c * 128
        matrix[:, c * 128 : (c + 1) * 128] = (column == source).astype(F32).astype(BF16)
    total[...] = (p0[...].astype(F32) + p1[...].astype(F32)) + (p2[...].astype(F32) + p3[...].astype(F32))
    for r in range(0, 32, 2):
        both = returned[r * 8 : r * 8 + 16, :].astype(F32)
        for u in range(2):
            asked = wanted[r + u, member]
            row = pl.multiple_of(jnp.clip(asked - member * 32, 0, 31) * 8, 8)

            @pl.when(asked >= 0)
            def _():
                total[pl.ds(row, 8), :] += both[u * 8 : (u + 1) * 8]

    value = total[...]
    high = value.astype(BF16)
    low = (value - high.astype(F32)).astype(BF16)
    out[...] = jnp.dot(high, matrix[...], preferred_element_type=F32) + jnp.dot(
        low, matrix[...], preferred_element_type=F32
    )


SMEM = pl.BlockSpec(memory_space=pltpu.SMEM)
VMEM = pl.BlockSpec(memory_space=pltpu.VMEM)


def call(kernel, name, ins, outs, scratch):
    return pl.pallas_call(
        kernel,
        name=name,
        in_specs=ins,
        out_specs=[spec for spec, _ in outs],
        out_shape=[shape for _, shape in outs],
        scratch_shapes=scratch,
        compiler_params=pltpu.CompilerParams(vmem_limit_bytes=60 << 20),
    )


def ring(slab):
    up = [(k, (k + 1) % 4) for k in range(4)]
    down = [(k, (k + 3) % 4) for k in range(4)]
    left = lax.ppermute(slab, "grp", up)
    right = lax.ppermute(slab, "grp", down)
    far_low = lax.ppermute(left[:128], "grp", up)
    far_high = lax.ppermute(right[128:], "grp", down)
    return (slab, left, right, far_low, far_high)


def scatter(parts):
    got = [parts[0]]
    for k in (1, 2, 3):
        got.append(lax.ppermute(parts[k], "grp", [(m, (m + k) % 4) for m in range(4)]))
    return got


def shards(orbitals, anchors, wanted, pairs, counts):
    blocks, along_x, inverse = (jnp.asarray(t) for t in tables())
    wanted = wanted.reshape(32, 32)
    slab_type = jax.ShapeDtypeStruct((256, PLANE), BF16)
    slab, outgoing = call(
        order_kernel, "order", [SMEM, VMEM], [(VMEM, slab_type)] * 2,
        [pltpu.VMEM((PLANE, PLANE), BF16), pltpu.VMEM((256, PLANE), F32)],
    )(wanted, orbitals.reshape(256, PLANE))
    own = ring(slab)
    incoming = lax.all_to_all(outgoing, "orb", split_axis=0, concat_axis=0, tiled=True)
    list_type = jax.ShapeDtypeStruct((LIST,), jnp.int32)
    own_list, far_list, totals = call(
        list_kernel, "lists", [SMEM] * 4,
        [(SMEM, list_type), (SMEM, list_type), (SMEM, jax.ShapeDtypeStruct((2,), jnp.int32))],
        [pltpu.SMEM((32 * 64,), jnp.int32)],
    )(pairs.reshape(4, -1), counts, wanted, anchors)
    far = ring(incoming)

    def work(total):
        return [
            pltpu.VMEM((total, CHUNKS, PAD, 128), F32),
            pltpu.VMEM((total, CHUNKS, PAD, 128), F32),
            pltpu.VMEM((4, BATCH * EXT, 256), BF16),
            pltpu.VMEM((4, BATCH * EXT, 256), F32),
        ]

    (before,) = call(
        own_kernel, "own", [SMEM] * 2 + [VMEM] * 8,
        [(VMEM, jax.ShapeDtypeStruct((32, CHUNKS, EXT, 128), F32))], work(32),
    )(totals, own_list, *own, blocks, along_x, inverse)
    parts = call(
        far_kernel, "far", [SMEM] * 2 + [VMEM] * 14, [(VMEM, slab_type)] * 8, work(64),
    )(totals, far_list, before, *own, *far, blocks, along_x, inverse)
    far_got = scatter(parts[4:])
    own_got = scatter(parts[:4])
    far_sum = sum(part.astype(F32) for part in far_got).astype(BF16)
    returned = lax.all_to_all(far_sum, "orb", split_axis=0, concat_axis=0, tiled=True)
    (result,) = call(
        finish_kernel, "finish", [SMEM] + [VMEM] * 5,
        [(VMEM, jax.ShapeDtypeStruct((256, PLANE), F32))],
        [pltpu.VMEM((PLANE, PLANE), BF16), pltpu.VMEM((256, PLANE), F32)],
    )(wanted, *own_got, returned)
    return result.reshape(32, 8, PLANE)


def solution(mesh):
    return jax.shard_map(
        shards,
        mesh=mesh,
        in_specs=(P("orb", "grp", None), P(), P(), P("orb", None, None, None), P("orb", None)),
        out_specs=P("orb", "grp", None),
        check_vma=False,
    )
```

time: 1090 us -> 199 us (0.18)
  local copies, waits for them, and re-layouts: 498 us -> 5.52 us
  other arithmetic: 279 us -> 2.2 us
  matrix products: 198 us -> 0 us
  Pallas kernels: 0 us -> 99.5 us
  starting transfers between devices: 7.88 us -> 43.6 us
  blocking collectives: 31.1 us -> 0 us
  between operations: 14.2 us -> 0.16 us
    convert_element_type x20 -> x0, local copies, waits for them, and re-layouts: 408 us -> none  [the longest x8 196 us: potential(): section_four = along_middle(section_three).astype(jnp.bfloat16)]
    scatter-add x13 -> x0, other arithmetic: 237 us -> none  [the longest x4 77.8 us: turn(): partner_sum = partner_sum.at[jnp.where(in_range & ~from_own, window(secon...]
    dot_general x28 -> x0, matrix products: 198 us -> none  [the longest x8 60.3 us: along_first(): jnp.einsum('kx,pxq->pkq', sine_rows, values, preferred_element_type=jnp.f...]
    pallas_call x0 -> x5, Pallas kernels: none -> 99.5 us  [the longest x1 46.6 us: shards(): call(list_kernel, 'lists', [SMEM] * 4, [(SMEM, list_type), (SMEM, list_ty...]
    gather x17 -> x0, local copies, waits for them, and re-layouts: 46.5 us -> none  [the longest x4 17.5 us: turn(): partner_full[window(second_slot)]]
    all_to_all x1 -> x0, blocking collectives: 31.1 us -> none  [shards(): lax.all_to_all(partner_acc.astype(jnp.bfloat16), 'orb', split_axis=0, con...]
    ppermute x0 -> x14, waiting for transfers between devices: none -> 30.8 us  [the longest x6 24.6 us: scatter(): lax.ppermute(parts[k], 'grp', [(m, (m + k) % 4) for m in range(4)])]
    all_gather x1 -> x0, waiting for transfers between devices: 28.7 us -> none  [shards(): own_full = lax.all_gather(slab_boxes, 'grp', axis=1, tiled=True)]
  transfers between devices with their start and end apart: 3 -> 16, of which waited for: 3 -> 8; matrix products, arithmetic and copies ran while one was open for 3% -> 3% of each run, Pallas kernels for 0% -> 34%
where the time goes in v1:
time: 199 us
  Pallas kernels  99.5 us (50%)
  waiting for transfers between devices  48.1 us (24%)
  starting transfers between devices  43.6 us (22%)
  local copies, waits for them, and re-layouts  5.52 us (3%)
  other arithmetic  2.2 us (1%)
    pallas_call x1, Pallas kernels, shards(): call(list_kernel, 'lists', [SMEM] * 4, [(SMEM, list_type), (SMEM, list_ty...  46.6 us
    ppermute x6, waiting for transfers between devices, scatter(): lax.ppermute(parts[k], 'grp', [(m, (m + k) % 4) for m in range(4)])  24.6 us
    pallas_call x1, Pallas kernels, shards(): call(far_kernel, 'far', [SMEM] * 2 + [VMEM] * 14, [(VMEM, slab_type)] * 8...  23 us
    pallas_call x1, Pallas kernels, shards(): call(own_kernel, 'own', [SMEM] * 2 + [VMEM] * 8, [(VMEM, jax.ShapeDtypeSt...  21.3 us
    all_to_all x1, starting transfers between devices, shards(): lax.all_to_all(far_sum, 'orb', split_axis=0, concat_axis=0, tiled=True)  15.4 us
    all_to_all x1, starting transfers between devices, shards(): lax.all_to_all(outgoing, 'orb', split_axis=0, concat_axis=0, tiled=True)  9.42 us
    all_to_all x1, waiting for transfers between devices, shards(): lax.all_to_all(far_sum, 'orb', split_axis=0, concat_axis=0, tiled=True)  8.67 us
    all_to_all x1, waiting for transfers between devices, shards(): lax.all_to_all(outgoing, 'orb', split_axis=0, concat_axis=0, tiled=True)  8.62 us
  transfers between devices with their start and end apart: 16, of which 8 were waited for; matrix products, arithmetic and copies ran while one was open for 3% of the time, Pallas kernels for 34%

profile of v1, /device:TPU:1, one launch (start us, length us, event | category | flops | bytes accessed | tf_op | source)
XLA Modules:
  0.0 199.2 jit_solution(8247368257612734608)
XLA Ops:
  0.0 3.3 %order.1 = (bf16[256,1024]{1,0:T(8,128)(2,1)}, bf16[256,1024]{1,0:T(8,128)(2,1)}) custom-call(s32[32,32]{1,0:T(8,128)} %bitcast.16, f32[256,1024]{1,0:T(8,128)} %bitcast.13), custom_call_target="tpu_custom_call" | custom-call | tf_op jit(solution)/shard_map/order/pallas_call | solution.py:305
  3.3 9.4 %all-to-all-start = ((bf16[32,8,1024]{2,1,0:T(8,128)(2,1)}), bf16[32,8,1024]{2,1,0:T(8,128)(2,1)S(1)}, u32[]{:S(2)}, u32[]{:S(2)}) async-start(bf16[32,8,1024]{2,1,0:T(8,128)(2,1)} %bitcast.15), calls=%async_computation | async-start | bytes 1048576 | tf_op jit(solution)/shard_map/all_to_all | solution.py:310
  12.7 2.8 %collective-permute-start.1 = (bf16[256,1024]{1,0:T(8,128)(2,1)}, bf16[256,1024]{1,0:T(8,128)(2,1)S(1)}, u32[]{:S(2)}, u32[]{:S(2)}) collective-permute-start(bf16[256,1024]{1,0:T(8,128)(2,1)} %get-tuple-element.21.s), channel_id=1, source_target_pairs={{0,3},{1,0},{2,1},{3,2},{4,7},{5,4},{6,5},{7,6},{8,11},{9,8},{10,9... | collective-permute-start | bytes 1572872 | tf_op jit(solution)/shard_map/ppermute | solution.py:288
  15.5 8.6 %all-to-all-done = bf16[32,8,1024]{2,1,0:T(8,128)(2,1)S(1)} async-done(((bf16[32,8,1024]{2,1,0:T(8,128)(2,1)}), bf16[32,8,1024]{2,1,0:T(8,128)(2,1)S(1)}, u32[]{:S(2)}, u32[]{:S(2)}) %all-to-all-start) | async-done | bytes 524320 | tf_op jit(solution)/shard_map/all_to_all | solution.py:310
  24.2 2.7 %collective-permute-start.5 = (bf16[256,1024]{1,0:T(8,128)(2,1)S(1)}, bf16[256,1024]{1,0:T(8,128)(2,1)S(1)}, u32[]{:S(2)}, u32[]{:S(2)}) collective-permute-start(bf16[256,1024]{1,0:T(8,128)(2,1)S(1)} %bitcast.9), channel_id=1, source_target_pairs={{0,3},{1,0},{2,1},{3,2},{4,7},{5,4},{6,5},{7,6},{8,11},{9,8},{10,9... | collective-permute-start | bytes 1572872 | tf_op jit(solution)/shard_map/ppermute | solution.py:288
  26.9 0.8 slice.17
  27.7 3.3 %collective-permute-start.3 = (bf16[128,1024]{1,0:T(8,128)(2,1)}, bf16[128,1024]{1,0:T(8,128)(2,1)S(1)}, u32[]{:S(2)}, u32[]{:S(2)}) collective-permute-start(bf16[128,1024]{1,0:T(8,128)(2,1)} %slice.17), channel_id=1, source_target_pairs={{0,3},{1,0},{2,1},{3,2},{4,7},{5,4},{6,5},{7,6},{8,11},{9,8},{10,9... | collective-permute-start | bytes 786440 | tf_op jit(solution)/shard_map/ppermute | solution.py:290
  31.0 0.8 slice.16
  31.7 6.2 %collective-permute-done.5.fl = bf16[256,1024]{1,0:T(8,128)(2,1)S(1)} collective-permute-done((bf16[256,1024]{1,0:T(8,128)(2,1)S(1)}, bf16[256,1024]{1,0:T(8,128)(2,1)S(1)}, u32[]{:S(2)}, u32[]{:S(2)}) %collective-permute-start.5) | collective-permute-done | bytes 524320 | tf_op jit(solution)/shard_map/ppermute | solution.py:288
  38.0 0.8 slice.19
  38.7 3.4 %collective-permute-start.7 = (bf16[128,1024]{1,0:T(8,128)(2,1)}, bf16[128,1024]{1,0:T(8,128)(2,1)}, u32[]{:S(2)}, u32[]{:S(2)}) collective-permute-start(bf16[128,1024]{1,0:T(8,128)(2,1)} %slice.19), channel_id=1, source_target_pairs={{0,3},{1,0},{2,1},{3,2},{4,7},{5,4},{6,5},{7,6},{8,11},{9,8},{10,9... | collective-permute-start | bytes 786440 | tf_op jit(solution)/shard_map/ppermute | solution.py:290
  42.1 0.8 slice.18
  42.9 0.2 copy.10
  43.1 0.7 copy.11.pairs
  43.8 46.6 %lists.1 = (s32[256]{0:T(256)}, s32[256]{0:T(256)}, s32[2]{0:T(128)}) custom-call(s32[4,480]{1,0:T(4,128)} %copy.11.pairs, s32[1,4]{1,0:T(1,128)} %counts.1, s32[32,32]{1,0:T(8,128)} %bitcast.17, s32[1024]{0:T(1024)} %anchors.1), custom_call_target="tpu_custom_call" | custom-call | tf_op jit(solution)/shard_map/lists/pallas_call | solution.py:312
  90.5 0.6 copy-done.6
  91.1 0.1 copy-done.7
  91.3 21.3 %own.1.before = f32[32,8,32,128]{3,2,1,0:T(8,128)} custom-call(s32[2]{0:T(128)} %get-tuple-element.18.totals, s32[256]{0:T(256)} %get-tuple-element.20.listed, bf16[256,1024]{1,0:T(8,128)(2,1)} %get-tuple-element.21.s, bf16[256,1024]{1,0:T(8,128)(2,1)} %copy-done.1, bf16[256,1024]{1,0:T(8,128)(2,1)} %copy-done, bf16[128,1024]{1,0:T(8,128)(2,1)} %copy-done.7, ...), custom_call_target="tpu_custom_call" | custom-call | tf_op jit(solution)/shard_map/own/pallas_call | solution.py:327
  112.6 23.0 %far.1 = (bf16[256,1024]{1,0:T(8,128)(2,1)}, bf16[256,1024]{1,0:T(8,128)(2,1)}, bf16[256,1024]{1,0:T(8,128)(2,1)}, bf16[256,1024]{1,0:T(8,128)(2,1)}, bf16[256,1...) custom-call(s32[2]{0:T(128)} %get-tuple-element.18.totals, ...), custom_call_target="tpu_custom_call" | custom-call | tf_op jit(solution)/shard_map/far/pallas_call | solution.py:331
  135.7 3.9 %collective-permute-start.12 = (bf16[256,1024]{1,0:T(8,128)(2,1)}, bf16[256,1024]{1,0:T(8,128)(2,1)S(1)}, u32[]{:S(2)}, u32[]{:S(2)}) collective-permute-start(bf16[256,1024]{1,0:T(8,128)(2,1)} %get-tuple-element.29), channel_id=1, source_target_pairs={{0,2},{1,3},{2,0},{3,1},{4,6},{5,7},{6,4},{7,5},{8,10},{9,11},{10,... | collective-permute-start | bytes 1572872 | tf_op jit(solution)/shard_map/ppermute | solution.py:297
  139.6 1.5 collective-permute-start.8
  141.0 7.5 %collective-permute-done.11 = bf16[256,1024]{1,0:T(8,128)(2,1)S(1)} collective-permute-done((bf16[256,1024]{1,0:T(8,128)(2,1)}, bf16[256,1024]{1,0:T(8,128)(2,1)S(1)}, u32[]{:S(2)}, u32[]{:S(2)}) %collective-permute-start.11) | collective-permute-done | bytes 524320 | tf_op jit(solution)/shard_map/ppermute | solution.py:297
  148.5 1.2 collective-permute-start.10
  149.7 11.0 %collective-permute-done.12 = bf16[256,1024]{1,0:T(8,128)(2,1)S(1)} collective-permute-done((bf16[256,1024]{1,0:T(8,128)(2,1)}, bf16[256,1024]{1,0:T(8,128)(2,1)S(1)}, u32[]{:S(2)}, u32[]{:S(2)}) %collective-permute-start.12) | collective-permute-done | bytes 524320 | tf_op jit(solution)/shard_map/ppermute | solution.py:297
  160.7 3.4 %collective-permute-done.13 = bf16[256,1024]{1,0:T(8,128)(2,1)S(1)} collective-permute-done((bf16[256,1024]{1,0:T(8,128)(2,1)}, bf16[256,1024]{1,0:T(8,128)(2,1)S(1)}, u32[]{:S(2)}, u32[]{:S(2)}) %collective-permute-start.13) | collective-permute-done | bytes 524320 | tf_op jit(solution)/shard_map/ppermute | solution.py:297
  164.1 2.2 %fusion = bf16[32,8,1024]{2,1,0:T(8,128)(2,1)} fusion(bf16[256,1024]{1,0:T(8,128)(2,1)S(1)} %collective-permute-done.13, bf16[256,1024]{1,0:T(8,128)(2,1)S(1)} %collective-permute-done.12, bf16[256,1024]{1,0:T(8,128)(2,1)S(1)} %collective-permute-done.11, bf16[256,1024]{1,0:T(8,128)(2,1)} %get-tuple-element.27), kind=kLoop, calls=%fused_computation.1 | loop fusion | flops 2097152 | bytes 2621440 | tf_op jit(solution)/shard_map/all_to_all | solution.py:337
  166.3 15.4 %all-to-all-start.1 = ((bf16[32,8,1024]{2,1,0:T(8,128)(2,1)}), bf16[32,8,1024]{2,1,0:T(8,128)(2,1)S(1)}, u32[]{:S(2)}, u32[]{:S(2)}) async-start(bf16[32,8,1024]{2,1,0:T(8,128)(2,1)} %fusion), calls=%async_computation.1 | async-start | bytes 1048576 | tf_op jit(solution)/shard_map/all_to_all | solution.py:337
  181.7 1.5 collective-permute-done.9.p2
  183.2 1.2 collective-permute-done.10.p3
  184.4 8.7 %all-to-all-done.1 = bf16[32,8,1024]{2,1,0:T(8,128)(2,1)S(1)} async-done(((bf16[32,8,1024]{2,1,0:T(8,128)(2,1)}), bf16[32,8,1024]{2,1,0:T(8,128)(2,1)S(1)}, u32[]{:S(2)}, u32[]{:S(2)}) %all-to-all-start.1) | async-done | bytes 524320 | tf_op jit(solution)/shard_map/all_to_all | solution.py:337
  193.1 0.8 copy-done.3
  193.9 5.3 %finish.1 = f32[256,1024]{1,0:T(8,128)} custom-call(s32[32,32]{1,0:T(8,128)} %bitcast.18, bf16[256,1024]{1,0:T(8,128)(2,1)} %get-tuple-element.23.p0, bf16[256,1024]{1,0:T(8,128)(2,1)} %copy-done.8, bf16[256,1024]{1,0:T(8,128)(2,1)} %copy-done.9, bf16[256,1024]{1,0:T(8,128)(2,1)} %copy-done.10, bf16[256,1024]{1,0:T(8,128)(2,1)} %bitcast.12), custom_call_target="tpu_custom_call" | custom-call | tf_op jit(solution)/shard_map/finish/pallas_call | solution.py:338
  (36 shorter events, 0.1 us)
Async XLA Ops:
  0.0 42.9 %copy-start.11 = (s32[1,4,240,2]{2,3,1,0:T(2,128)S(1)}, s32[1,4,240,2]{2,3,1,0:T(2,128)}, u32[]{:S(2)}) copy-start(s32[1,4,240,2]{2,3,1,0:T(2,128)} %param.11) | copy-start | bytes 23044
  3.3 20.9 %all-to-all-start = ((bf16[32,8,1024]{2,1,0:T(8,128)(2,1)}), bf16[32,8,1024]{2,1,0:T(8,128)(2,1)S(1)}, u32[]{:S(2)}, u32[]{:S(2)}) async-start(bf16[32,8,1024]{2,1,0:T(8,128)(2,1)} %bitcast.15), calls=%async_computation | async-start | bytes 1048576 | tf_op jit(solution)/shard_map/all_to_all | solution.py:310
  12.7 14.2 %collective-permute-start.1 = (bf16[256,1024]{1,0:T(8,128)(2,1)}, bf16[256,1024]{1,0:T(8,128)(2,1)S(1)}, u32[]{:S(2)}, u32[]{:S(2)}) collective-permute-start(bf16[256,1024]{1,0:T(8,128)(2,1)} %get-tuple-element.21.s), channel_id=1, source_target_pairs={{0,3},{1,0},{2,1},{3,2},{4,7},{5,4},{6,5},{7,6},{8,11},{9,8},{10,9... | collective-permute-start | bytes 1572872 | tf_op jit(solution)/shard_map/ppermute | solution.py:288
  15.5 15.4 %collective-permute-start = (bf16[256,1024]{1,0:T(8,128)(2,1)}, bf16[256,1024]{1,0:T(8,128)(2,1)S(1)}, u32[]{:S(2)}, u32[]{:S(2)}) collective-permute-start(bf16[256,1024]{1,0:T(8,128)(2,1)} %get-tuple-element.21.s), channel_id=1, source_target_pairs={{0,1},{1,2},{2,3},{3,0},{4,5},{5,6},{6,7},{7,4},{8,9},{9,10},{10,1... | collective-permute-start | bytes 1572872 | tf_op jit(solution)/shard_map/ppermute | solution.py:287
  24.2 88.4 %copy-start.2 = (bf16[32,8,1024]{2,1,0:T(8,128)(2,1)}, bf16[32,8,1024]{2,1,0:T(8,128)(2,1)S(1)}, u32[]{:S(2)}) copy-start(bf16[32,8,1024]{2,1,0:T(8,128)(2,1)S(1)} %all-to-all-done) | copy-start | bytes 1572868
  24.2 13.8 %collective-permute-start.5 = (bf16[256,1024]{1,0:T(8,128)(2,1)S(1)}, bf16[256,1024]{1,0:T(8,128)(2,1)S(1)}, u32[]{:S(2)}, u32[]{:S(2)}) collective-permute-start(bf16[256,1024]{1,0:T(8,128)(2,1)S(1)} %bitcast.9), channel_id=1, source_target_pairs={{0,3},{1,0},{2,1},{3,2},{4,7},{5,4},{6,5},{7,6},{8,11},{9,8},{10,9... | collective-permute-start | bytes 1572872 | tf_op jit(solution)/shard_map/ppermute | solution.py:288
  26.9 15.2 %collective-permute-start.4 = (bf16[256,1024]{1,0:T(8,128)(2,1)S(1)}, bf16[256,1024]{1,0:T(8,128)(2,1)S(1)}, u32[]{:S(2)}, u32[]{:S(2)}) collective-permute-start(bf16[256,1024]{1,0:T(8,128)(2,1)S(1)} %bitcast.10), channel_id=1, source_target_pairs={{0,1},{1,2},{2,3},{3,0},{4,5},{5,6},{6,7},{7,4},{8,9},{9,10},{10,1... | collective-permute-start | bytes 1572872 | tf_op jit(solution)/shard_map/ppermute | solution.py:287
  26.9 63.6 %copy-start = (bf16[256,1024]{1,0:T(8,128)(2,1)}, bf16[256,1024]{1,0:T(8,128)(2,1)S(1)}, u32[]{:S(2)}) copy-start(bf16[256,1024]{1,0:T(8,128)(2,1)S(1)} %collective-permute-done.1.l) | copy-start | bytes 1572868
  27.7 62.8 %collective-permute-start.3 = (bf16[128,1024]{1,0:T(8,128)(2,1)}, bf16[128,1024]{1,0:T(8,128)(2,1)S(1)}, u32[]{:S(2)}, u32[]{:S(2)}) collective-permute-start(bf16[128,1024]{1,0:T(8,128)(2,1)} %slice.17), channel_id=1, source_target_pairs={{0,3},{1,0},{2,1},{3,2},{4,7},{5,4},{6,5},{7,6},{8,11},{9,8},{10,9... | collective-permute-start | bytes 786440 | tf_op jit(solution)/shard_map/ppermute | solution.py:290
  31.0 59.5 %copy-start.1 = (bf16[256,1024]{1,0:T(8,128)(2,1)}, bf16[256,1024]{1,0:T(8,128)(2,1)S(1)}, u32[]{:S(2)}) copy-start(bf16[256,1024]{1,0:T(8,128)(2,1)S(1)} %collective-permute-done.r) | copy-start | bytes 1572868
  31.7 58.7 %collective-permute-start.2 = (bf16[128,1024]{1,0:T(8,128)(2,1)}, bf16[128,1024]{1,0:T(8,128)(2,1)S(1)}, u32[]{:S(2)}, u32[]{:S(2)}) collective-permute-start(bf16[128,1024]{1,0:T(8,128)(2,1)} %slice.16), channel_id=1, source_target_pairs={{0,1},{1,2},{2,3},{3,0},{4,5},{5,6},{6,7},{7,4},{8,9},{9,10},{10,1... | collective-permute-start | bytes 786440 | tf_op jit(solution)/shard_map/ppermute | solution.py:289
  38.0 74.6 %copy-start.4 = (bf16[256,1024]{1,0:T(8,128)(2,1)}, bf16[256,1024]{1,0:T(8,128)(2,1)S(1)}, u32[]{:S(2)}) copy-start(bf16[256,1024]{1,0:T(8,128)(2,1)S(1)} %collective-permute-done.5.fl) | copy-start | bytes 1572868
  38.7 73.9 %collective-permute-start.7 = (bf16[128,1024]{1,0:T(8,128)(2,1)}, bf16[128,1024]{1,0:T(8,128)(2,1)}, u32[]{:S(2)}, u32[]{:S(2)}) collective-permute-start(bf16[128,1024]{1,0:T(8,128)(2,1)} %slice.19), channel_id=1, source_target_pairs={{0,3},{1,0},{2,1},{3,2},{4,7},{5,4},{6,5},{7,6},{8,11},{9,8},{10,9... | collective-permute-start | bytes 786440 | tf_op jit(solution)/shard_map/ppermute | solution.py:290
  42.1 70.5 %copy-start.5 = (bf16[256,1024]{1,0:T(8,128)(2,1)}, bf16[256,1024]{1,0:T(8,128)(2,1)S(1)}, u32[]{:S(2)}) copy-start(bf16[256,1024]{1,0:T(8,128)(2,1)S(1)} %collective-permute-done.4.fr) | copy-start | bytes 1572868
  42.9 69.7 %collective-permute-start.6 = (bf16[128,1024]{1,0:T(8,128)(2,1)}, bf16[128,1024]{1,0:T(8,128)(2,1)}, u32[]{:S(2)}, u32[]{:S(2)}) collective-permute-start(bf16[128,1024]{1,0:T(8,128)(2,1)} %slice.18), channel_id=1, source_target_pairs={{0,1},{1,2},{2,3},{3,0},{4,5},{5,6},{6,7},{7,4},{8,9},{9,10},{10,1... | collective-permute-start | bytes 786440 | tf_op jit(solution)/shard_map/ppermute | solution.py:289
  90.4 0.7 copy-start.6
  90.5 0.8 copy-start.7
  135.6 12.9 %collective-permute-start.11 = (bf16[256,1024]{1,0:T(8,128)(2,1)}, bf16[256,1024]{1,0:T(8,128)(2,1)S(1)}, u32[]{:S(2)}, u32[]{:S(2)}) collective-permute-start(bf16[256,1024]{1,0:T(8,128)(2,1)} %get-tuple-element.28), channel_id=1, source_target_pairs={{0,1},{1,2},{2,3},{3,0},{4,5},{5,6},{6,7},{7,4},{8,9},{9,10},{10,1... | collective-permute-start | bytes 1572872 | tf_op jit(solution)/shard_map/ppermute | solution.py:297
  135.7 25.0 %collective-permute-start.12 = (bf16[256,1024]{1,0:T(8,128)(2,1)}, bf16[256,1024]{1,0:T(8,128)(2,1)S(1)}, u32[]{:S(2)}, u32[]{:S(2)}) collective-permute-start(bf16[256,1024]{1,0:T(8,128)(2,1)} %get-tuple-element.29), channel_id=1, source_target_pairs={{0,2},{1,3},{2,0},{3,1},{4,6},{5,7},{6,4},{7,5},{8,10},{9,11},{10,... | collective-permute-start | bytes 1572872 | tf_op jit(solution)/shard_map/ppermute | solution.py:297
  139.6 24.5 %collective-permute-start.13 = (bf16[256,1024]{1,0:T(8,128)(2,1)}, bf16[256,1024]{1,0:T(8,128)(2,1)S(1)}, u32[]{:S(2)}, u32[]{:S(2)}) collective-permute-start(bf16[256,1024]{1,0:T(8,128)(2,1)} %get-tuple-element.30), channel_id=1, source_target_pairs={{0,3},{1,0},{2,1},{3,2},{4,7},{5,4},{6,5},{7,6},{8,11},{9,8},{10,9... | collective-permute-start | bytes 1572872 | tf_op jit(solution)/shard_map/ppermute | solution.py:297
  139.6 42.1 %collective-permute-start.8 = (bf16[256,1024]{1,0:T(8,128)(2,1)}, bf16[256,1024]{1,0:T(8,128)(2,1)S(1)}, u32[]{:S(2)}, u32[]{:S(2)}) collective-permute-start(bf16[256,1024]{1,0:T(8,128)(2,1)} %get-tuple-element.24), channel_id=1, source_target_pairs={{0,1},{1,2},{2,3},{3,0},{4,5},{5,6},{6,7},{7,4},{8,9},{9,10},{10,1... | collective-permute-start | bytes 1572872 | tf_op jit(solution)/shard_map/ppermute | solution.py:297
  141.0 42.2 %collective-permute-start.9 = (bf16[256,1024]{1,0:T(8,128)(2,1)}, bf16[256,1024]{1,0:T(8,128)(2,1)S(1)}, u32[]{:S(2)}, u32[]{:S(2)}) collective-permute-start(bf16[256,1024]{1,0:T(8,128)(2,1)} %get-tuple-element.25), channel_id=1, source_target_pairs={{0,2},{1,3},{2,0},{3,1},{4,6},{5,7},{6,4},{7,5},{8,10},{9,11},{10,... | collective-permute-start | bytes 1572872 | tf_op jit(solution)/shard_map/ppermute | solution.py:297
  148.5 35.9 %collective-permute-start.10 = (bf16[256,1024]{1,0:T(8,128)(2,1)}, bf16[256,1024]{1,0:T(8,128)(2,1)S(1)}, u32[]{:S(2)}, u32[]{:S(2)}) collective-permute-start(bf16[256,1024]{1,0:T(8,128)(2,1)} %get-tuple-element.26), channel_id=1, source_target_pairs={{0,3},{1,0},{2,1},{3,2},{4,7},{5,4},{6,5},{7,6},{8,11},{9,8},{10,9... | collective-permute-start | bytes 1572872 | tf_op jit(solution)/shard_map/ppermute | solution.py:297
  166.3 26.8 %all-to-all-start.1 = ((bf16[32,8,1024]{2,1,0:T(8,128)(2,1)}), bf16[32,8,1024]{2,1,0:T(8,128)(2,1)S(1)}, u32[]{:S(2)}, u32[]{:S(2)}) async-start(bf16[32,8,1024]{2,1,0:T(8,128)(2,1)} %fusion), calls=%async_computation.1 | async-start | bytes 1048576 | tf_op jit(solution)/shard_map/all_to_all | solution.py:337
  181.7 11.4 %copy-start.8 = (bf16[256,1024]{1,0:T(8,128)(2,1)}, bf16[256,1024]{1,0:T(8,128)(2,1)S(1)}, u32[]{:S(2)}) copy-start(bf16[256,1024]{1,0:T(8,128)(2,1)S(1)} %collective-permute-done.8.p1) | copy-start | bytes 1572868
  183.2 9.9 %copy-start.9 = (bf16[256,1024]{1,0:T(8,128)(2,1)}, bf16[256,1024]{1,0:T(8,128)(2,1)S(1)}, u32[]{:S(2)}) copy-start(bf16[256,1024]{1,0:T(8,128)(2,1)S(1)} %collective-permute-done.9.p2) | copy-start | bytes 1572868
  184.4 8.7 %copy-start.10 = (bf16[256,1024]{1,0:T(8,128)(2,1)}, bf16[256,1024]{1,0:T(8,128)(2,1)S(1)}, u32[]{:S(2)}) copy-start(bf16[256,1024]{1,0:T(8,128)(2,1)S(1)} %collective-permute-done.10.p3) | copy-start | bytes 1572868
  193.1 0.8 copy-start.3

commit v2 on v1

--- a/solution.py
+++ b/solution.py
@@ -66,56 +66,50 @@
         outgoing[r * 8 : r * 8 + 16, :] = jnp.concatenate([low, high], axis=0).astype(BF16)
 
 
-def list_kernel(pairs, counts, wanted, anchors, own_list, far_list, totals, table):
+def list_kernel(counts, pairs, wanted, own_list, far_list):
     member = lax.axis_index("orb")
     position = lax.axis_index("grp")
-
-    def clear(k, carry):
-        for u in range(16):
-            table[k * 16 + u] = 0
-        return carry
-
-    lax.fori_loop(0, 32 * 64 // 16, clear, 0)
-
-    def blank(k, carry):
-        for u in range(8):
-            own_list[k * 8 + u] = MARGIN << 11
-            far_list[k * 8 + u] = MARGIN << 11
-        return carry
-
-    lax.fori_loop(0, LIST // 8, blank, 0)
+    weights = jnp.zeros((64, 32), F32)
+    slot = lax.broadcasted_iota(jnp.int32, (1, 240), 1)
     for g in range(4):
-
-        def note(p, carry):
-            cell = (pairs[g, p * 2] & 31) * 64 + pairs[g, p * 2 + 1]
-            table[cell] = table[cell] + 1
-            return carry
-
-        lax.fori_loop(0, counts[0, g], note, 0)
-
-    def collect(first, target):
-        def one(k, found):
-            i = k >> 5
-            c = (k & 31) + first
-            weight = table[i * 64 + c]
-            if first:
-                other = wanted[member, c - 32]
-            else:
-                other = member * 32 + c
-            live = (weight > 0) & (other >= 0)
-
-            @pl.when(live & ((found & 3) == position))
-            def _():
-                d = anchors[jnp.maximum(other, 0)] - anchors[member * 32 + i]
-                target[found >> 2] = i | (c << 5) | ((d + MARGIN) << 11) | (weight << 16)
-
-            return found + live.astype(jnp.int32)
-
-        found = lax.fori_loop(0, 32 * 32, one, 0)
-        return (found - position + 3) >> 2
-
-    totals[0] = collect(0, own_list)
-    totals[1] = collect(32, far_list)
+        live = slot < counts[0, g]
+        first = jnp.where(live, pairs[g, 0:1, :] & 31, -1)
+        code = jnp.where(live, pairs[g, 1:2, :], -1)
+        first_hot = (lax.broadcasted_iota(jnp.int32, (32, 240), 0) == first).astype(F32).astype(BF16)
+        code_hot = (lax.broadcasted_iota(jnp.int32, (64, 240), 0) == code).astype(F32).astype(BF16)
+        weights += lax.dot_general(code_hot, first_hot, (((1,), (1,)), ((), ())), preferred_element_type=F32)
+    down = lax.broadcasted_iota(jnp.int32, (32, 32), 0)
+    across = lax.broadcasted_iota(jnp.int32, (32, 32), 1)
+    asked = jnp.where(down == across, wanted[pl.ds(member, 1), :], 0)
+    asked = jnp.sum(asked.astype(F32), axis=1, keepdims=True) >= 0.0
+    lower = (across <= down).astype(F32).astype(BF16)
+    before = (down < across).astype(F32).astype(BF16)
+    lane = lax.broadcasted_iota(jnp.int32, (1, LIST), 1)
+    for half, target in ((0, own_list), (1, far_list)):
+        weight = weights[half * 32 : half * 32 + 32]
+        live = weight > 0.5
+        if half:
+            live = live & asked
+        mask = live.astype(F32)
+        inner = jnp.dot(lower, mask.astype(BF16), preferred_element_type=F32)
+        total = jnp.broadcast_to(inner[31:32], (8, 32))
+        outer = jnp.dot(total.astype(BF16), before, preferred_element_type=F32)[0:1]
+        rank = (outer + inner).astype(jnp.int32) - 1
+        key = jnp.where(live & ((rank & 3) == position), rank >> 2, -1)
+        entry = across | (down << 5) | (weight.astype(jnp.int32) << 11)
+        found = jnp.zeros((32, LIST), jnp.int32)
+        for i in range(32):
+            found += jnp.where(key[:, i : i + 1] == lane, entry[:, i : i + 1], 0)
+        packed = jnp.sum(found, axis=0, keepdims=True)
+        every = jnp.sum(total[0:1], axis=1, keepdims=True).astype(jnp.int32)
+        target[...] = jnp.where(lane == LIST - 1, (every - position + 3) >> 2, packed)
+
+
+def make_lists(counts, pairs, wanted):
+    list_type = jax.ShapeDtypeStruct((1, LIST), jnp.int32)
+    return call(
+        list_kernel, "lists", [SMEM, VMEM, VMEM], [(VMEM, list_type)] * 2, [],
+    )(counts, jnp.transpose(pairs[0], (0, 2, 1)), wanted)
 
 
 def unpack_slab(block, rows, boxes, base, member_of):
@@ -140,13 +134,23 @@
     unpack_slab(far_high, 128, boxes, base + 16, (position + 2) & 3)
 
 
-def run_pairs(count, listed, boxes, sums, blocks, along_x, inverse, density, field):
+def run_pairs(base, anchors, wanted, listed, boxes, sums, blocks, along_x, inverse, density, field):
+    member = lax.axis_index("orb")
+    count = listed[0, LIST - 1]
+
     def fields(entry):
-        return (entry & 31, (entry >> 5) & 63, MARGIN + MARGIN - ((entry >> 11) & 31), entry >> 16)
+        i = entry & 31
+        c = (entry >> 5) & 31
+        if base:
+            other = jnp.maximum(wanted[member, c], 0)
+        else:
+            other = member * 32 + c
+        shifted = MARGIN + anchors[member * 32 + i] - anchors[other]
+        return (i, base + c, shifted, entry >> 11)
 
     def batch(b, carry):
         for p in range(BATCH):
-            i, j, shifted, weight = fields(listed[b * BATCH + p])
+            i, j, shifted, weight = fields(listed[0, b * BATCH + p])
             for h in range(2):
                 f = []
                 for q in range(4):
@@ -163,7 +167,7 @@
             t = jnp.dot(along_x[...], t, preferred_element_type=F32).astype(BF16)
             field[q] = lax.dot_general(t, blocks[q], (((1,), (1,)), ((), ())), preferred_element_type=F32)
         for p in range(BATCH):
-            i, j, shifted, weight = fields(listed[b * BATCH + p])
+            i, j, shifted, weight = fields(listed[0, b * BATCH + p])
             scale = weight.astype(F32)
             for h in range(2):
                 ee, eo, oe, oo = (
@@ -188,11 +192,11 @@
     lax.fori_loop(0, last - first, one, 0)
 
 
-def own_kernel(totals, listed, s, r, l, r2, l2, blocks, along_x, inverse, out, boxes, sums, density, field):
+def own_kernel(anchors, wanted, listed, s, r, l, r2, l2, blocks, along_x, inverse, out, boxes, sums, density, field):
     clear_rows(boxes, 0, 32)
     clear_rows(sums, 0, 32)
     fill((s, r, l, r2, l2), boxes, 0)
-    run_pairs(totals[0], listed, boxes, sums, blocks, along_x, inverse, density, field)
+    run_pairs(0, anchors, wanted, listed, boxes, sums, blocks, along_x, inverse, density, field)
 
     def one(k, carry):
         for c in range(CHUNKS):
@@ -204,24 +208,25 @@
 
 def pack_sums(sums, base, outs):
     position = lax.axis_index("grp")
-    for step in range(4):
+    own, ahead, low, high, behind = outs
+    for step, first, target in ((2, 0, low), (2, 16, high), (1, 0, ahead), (3, 0, behind), (0, 0, own)):
         start = pl.multiple_of(MARGIN + 8 * ((position + step) & 3), 8)
 
         def one(k, carry):
             for c in range(CHUNKS):
-                part = sums[pl.ds(base + 2 * k, 2), c, pl.ds(start, 8), :].reshape(16, 128)
-                outs[step][pl.ds(k * 16, 16), c * 128 : (c + 1) * 128] = part.astype(BF16)
+                part = sums[pl.ds(base + first + 2 * k, 2), c, pl.ds(start, 8), :].reshape(16, 128)
+                target[pl.ds(k * 16, 16), c * 128 : (c + 1) * 128] = part.astype(BF16)
             return carry
 
-        lax.fori_loop(0, 16, one, 0)
+        lax.fori_loop(0, target.shape[0] // 16, one, 0)
 
 
 def far_kernel(
-    totals, listed, before,
+    anchors, wanted, listed, before,
     s, r, l, r2, l2,
     fs, fr, fl, fr2, fl2,
     blocks, along_x, inverse,
-    o0, o1, o2, o3, f0, f1, f2, f3,
+    o0, o1, o2, o3, o4, f0, f1, f2, f3, f4,
     boxes, sums, density, field,
 ):
     clear_rows(boxes, 0, 64)
@@ -235,18 +240,18 @@
         return carry
 
     lax.fori_loop(0, 32, one, 0)
-    run_pairs(totals[1], listed, boxes, sums, blocks, along_x, inverse, density, field)
-    pack_sums(sums, 0, (o0, o1, o2, o3))
-    pack_sums(sums, 32, (f0, f1, f2, f3))
-
-
-def finish_kernel(wanted, p0, p1, p2, p3, returned, out, matrix, total):
+    run_pairs(32, anchors, wanted, listed, boxes, sums, blocks, along_x, inverse, density, field)
+    pack_sums(sums, 32, (f0, f1, f2, f3, f4))
+    pack_sums(sums, 0, (o0, o1, o2, o3, o4))
+
+
+def finish_kernel(wanted, p0, p1, p2, returned, out, matrix, total):
     member = lax.axis_index("orb")
     for c in range(CHUNKS):
         source = source_of(lax.broadcasted_iota(jnp.int32, (PLANE, 128), 0))
         column = lax.broadcasted_iota(jnp.int32, (PLANE, 128), 1) + c * 128
         matrix[:, c * 128 : (c + 1) * 128] = (column == source).astype(F32).astype(BF16)
-    total[...] = (p0[...].astype(F32) + p1[...].astype(F32)) + (p2[...].astype(F32) + p3[...].astype(F32))
+    total[...] = p0[...].astype(F32) + p1[...].astype(F32) + p2[...].astype(F32)
     for r in range(0, 32, 2):
         both = returned[r * 8 : r * 8 + 16, :].astype(F32)
         for u in range(2):
@@ -292,10 +297,18 @@
 
 
 def scatter(parts):
-    got = [parts[0]]
-    for k in (1, 2, 3):
-        got.append(lax.ppermute(parts[k], "grp", [(m, (m + k) % 4) for m in range(4)]))
-    return got
+    up = [(k, (k + 1) % 4) for k in range(4)]
+    down = [(k, (k + 3) % 4) for k in range(4)]
+    own, ahead, low, high, behind = parts
+    low = lax.ppermute(low, "grp", up)
+    high = lax.ppermute(high, "grp", down)
+
+    def add(a, b):
+        return (a.astype(F32) + b.astype(F32)).astype(BF16)
+
+    ahead = jnp.concatenate([add(ahead[:128], low), ahead[128:]], axis=0)
+    behind = jnp.concatenate([behind[:128], add(behind[128:], high)], axis=0)
+    return (own, lax.ppermute(ahead, "grp", up), lax.ppermute(behind, "grp", down))
 
 
 def shards(orbitals, anchors, wanted, pairs, counts):
@@ -308,12 +321,7 @@
     )(wanted, orbitals.reshape(256, PLANE))
     own = ring(slab)
     incoming = lax.all_to_all(outgoing, "orb", split_axis=0, concat_axis=0, tiled=True)
-    list_type = jax.ShapeDtypeStruct((LIST,), jnp.int32)
-    own_list, far_list, totals = call(
-        list_kernel, "lists", [SMEM] * 4,
-        [(SMEM, list_type), (SMEM, list_type), (SMEM, jax.ShapeDtypeStruct((2,), jnp.int32))],
-        [pltpu.SMEM((32 * 64,), jnp.int32)],
-    )(pairs.reshape(4, -1), counts, wanted, anchors)
+    own_list, far_list = make_lists(counts, pairs, wanted)
     far = ring(incoming)
 
     def work(total):
@@ -325,18 +333,20 @@
         ]
 
     (before,) = call(
-        own_kernel, "own", [SMEM] * 2 + [VMEM] * 8,
+        own_kernel, "own", [SMEM] * 3 + [VMEM] * 8,
         [(VMEM, jax.ShapeDtypeStruct((32, CHUNKS, EXT, 128), F32))], work(32),
-    )(totals, own_list, *own, blocks, along_x, inverse)
+    )(anchors, wanted, own_list, *own, blocks, along_x, inverse)
+    half_type = jax.ShapeDtypeStruct((128, PLANE), BF16)
+    packed = [(VMEM, t) for t in (slab_type, slab_type, half_type, half_type, slab_type)]
     parts = call(
-        far_kernel, "far", [SMEM] * 2 + [VMEM] * 14, [(VMEM, slab_type)] * 8, work(64),
-    )(totals, far_list, before, *own, *far, blocks, along_x, inverse)
-    far_got = scatter(parts[4:])
-    own_got = scatter(parts[:4])
+        far_kernel, "far", [SMEM] * 3 + [VMEM] * 14, packed * 2, work(64),
+    )(anchors, wanted, far_list, before, *own, *far, blocks, along_x, inverse)
+    far_got = scatter(parts[5:])
+    own_got = scatter(parts[:5])
     far_sum = sum(part.astype(F32) for part in far_got).astype(BF16)
     returned = lax.all_to_all(far_sum, "orb", split_axis=0, concat_axis=0, tiled=True)
     (result,) = call(
-        finish_kernel, "finish", [SMEM] + [VMEM] * 5,
+        finish_kernel, "finish", [SMEM] + [VMEM] * 4,
         [(VMEM, jax.ShapeDtypeStruct((256, PLANE), F32))],
         [pltpu.VMEM((PLANE, PLANE), BF16), pltpu.VMEM((256, PLANE), F32)],
     )(wanted, *own_got, returned)

time: 199 us -> 160 us (0.80)
  Pallas kernels: 99.5 us -> 57.9 us
  local copies, waits for them, and re-layouts: 5.52 us -> 8.5 us
  starting transfers between devices: 43.6 us -> 41.6 us
    pallas_call x4, Pallas kernels: 96.2 us -> 54.6 us  [the longest x1 25.8 us: shards(): call(far_kernel, 'far', [SMEM] * 3 + [VMEM] * 14, packed * 2, work(64))]
    ppermute x6 -> x8, waiting for transfers between devices: 24.6 us -> 19.3 us  [the longest x2 10.3 us: scatter(): lax.ppermute(ahead, 'grp', up)]
    all_to_all x1, starting transfers between devices: 15.4 us -> 10.2 us  [shards(): lax.all_to_all(far_sum, 'orb', split_axis=0, concat_axis=0, tiled=True)]
    slice x0 -> x4, local copies, waits for them, and re-layouts: none -> 3.93 us  [the longest x2 1.99 us: scatter(): ahead = jnp.concatenate([add(ahead[:128], low), ahead[128:]], axis=0)]
    ppermute x6 -> x8, starting transfers between devices: 6.59 us -> 9.64 us  [the longest x2 5.17 us: scatter(): lax.ppermute(behind, 'grp', down)]
    all_to_all x1, waiting for transfers between devices: 8.67 us -> 11.4 us  [shards(): lax.all_to_all(far_sum, 'orb', split_axis=0, concat_axis=0, tiled=True)]
    convert_element_type x0 -> x4, other arithmetic: none -> 2.16 us  [add(): return (a.astype(F32) + b.astype(F32)).astype(BF16)]
  transfers between devices with their start and end apart: 16 -> 18, of which waited for: 8 -> 8; matrix products, arithmetic and copies ran while one was open for 3% -> 6% of each run, Pallas kernels for 34% -> 15%
where the time goes in v2:
time: 160 us; the launch traced here: 159 us
  Pallas kernels  57.9 us (36%)
  waiting for transfers between devices  47.7 us (30%)
  starting transfers between devices  41.6 us (26%)
  local copies, waits for them, and re-layouts  8.5 us (5%)
  other arithmetic  3.37 us (2%)
    pallas_call x1, Pallas kernels, shards(): call(far_kernel, 'far', [SMEM] * 3 + [VMEM] * 14, packed * 2, work(64))  25.8 us
    pallas_call x1, Pallas kernels, shards(): call(own_kernel, 'own', [SMEM] * 3 + [VMEM] * 8, [(VMEM, jax.ShapeDtypeSt...  21.4 us
    all_to_all x1, waiting for transfers between devices, shards(): lax.all_to_all(far_sum, 'orb', split_axis=0, concat_axis=0, tiled=True)  11.4 us
    ppermute x2, waiting for transfers between devices, scatter(): lax.ppermute(ahead, 'grp', up)  10.3 us
    all_to_all x1, starting transfers between devices, shards(): lax.all_to_all(far_sum, 'orb', split_axis=0, concat_axis=0, tiled=True)  10.2 us
    all_to_all x1, starting transfers between devices, shards(): lax.all_to_all(outgoing, 'orb', split_axis=0, concat_axis=0, tiled=True)  9.42 us
    all_to_all x1, waiting for transfers between devices, shards(): lax.all_to_all(outgoing, 'orb', split_axis=0, concat_axis=0, tiled=True)  8.63 us
    ppermute x2, waiting for transfers between devices, scatter(): low = lax.ppermute(low, 'grp', up)  8.23 us
  transfers between devices with their start and end apart: 18, of which 8 were waited for; matrix products, arithmetic and copies ran while one was open for 6% of the time, Pallas kernels for 15%

profile of v2, /device:TPU:1, one launch (start us, length us, event | category | flops | bytes accessed | tf_op | source)
XLA Modules:
  0.0 159.2 jit_solution(2304123033177619779)
XLA Ops:
  0.0 3.3 %order.1 = (bf16[256,1024]{1,0:T(8,128)(2,1)}, bf16[256,1024]{1,0:T(8,128)(2,1)}) custom-call(s32[32,32]{1,0:T(8,128)} %bitcast.17, f32[256,1024]{1,0:T(8,128)} %bitcast.15), custom_call_target="tpu_custom_call" | custom-call | tf_op jit(solution)/shard_map/order/pallas_call | solution.py:318
  3.3 9.4 %all-to-all-start = ((bf16[32,8,1024]{2,1,0:T(8,128)(2,1)}), bf16[32,8,1024]{2,1,0:T(8,128)(2,1)S(1)}, u32[]{:S(2)}, u32[]{:S(2)}) async-start(bf16[32,8,1024]{2,1,0:T(8,128)(2,1)} %bitcast.16), calls=%async_computation | async-start | bytes 1048576 | tf_op jit(solution)/shard_map/all_to_all | solution.py:323
  12.7 2.8 %collective-permute-start.1 = (bf16[256,1024]{1,0:T(8,128)(2,1)}, bf16[256,1024]{1,0:T(8,128)(2,1)S(1)}, u32[]{:S(2)}, u32[]{:S(2)}) collective-permute-start(bf16[256,1024]{1,0:T(8,128)(2,1)} %get-tuple-element.21.s), channel_id=1, source_target_pairs={{0,3},{1,0},{2,1},{3,2},{4,7},{5,4},{6,5},{7,6},{8,11},{9,8},{10,9... | collective-permute-start | bytes 1572872 | tf_op jit(solution)/shard_map/ppermute | solution.py:293
  15.5 8.6 %all-to-all-done = bf16[32,8,1024]{2,1,0:T(8,128)(2,1)S(1)} async-done(((bf16[32,8,1024]{2,1,0:T(8,128)(2,1)}), bf16[32,8,1024]{2,1,0:T(8,128)(2,1)S(1)}, u32[]{:S(2)}, u32[]{:S(2)}) %all-to-all-start) | async-done | bytes 524320 | tf_op jit(solution)/shard_map/all_to_all | solution.py:323
  24.1 2.7 %collective-permute-start.5 = (bf16[256,1024]{1,0:T(8,128)(2,1)S(1)}, bf16[256,1024]{1,0:T(8,128)(2,1)S(1)}, u32[]{:S(2)}, u32[]{:S(2)}) collective-permute-start(bf16[256,1024]{1,0:T(8,128)(2,1)S(1)} %bitcast.11), channel_id=1, source_target_pairs={{0,3},{1,0},{2,1},{3,2},{4,7},{5,4},{6,5},{7,6},{8,11},{9,8},{10,9... | collective-permute-start | bytes 1572872 | tf_op jit(solution)/shard_map/ppermute | solution.py:293
  26.9 3.4 %collective-permute-start.3 = (bf16[128,1024]{1,0:T(8,128)(2,1)S(1)}, bf16[128,1024]{1,0:T(8,128)(2,1)S(1)}, u32[]{:S(2)}, u32[]{:S(2)}) collective-permute-start(bf16[128,1024]{1,0:T(8,128)(2,1)S(1)} %slice.49), channel_id=1, source_target_pairs={{0,3},{1,0},{2,1},{3,2},{4,7},{5,4},{6,5},{7,6},{8,11},{9,8},{10,9... | collective-permute-start | bytes 786440 | tf_op jit(solution)/shard_map/ppermute | solution.py:295
  30.3 0.8 slice.48
  31.0 6.9 %collective-permute-done.5.fl = bf16[256,1024]{1,0:T(8,128)(2,1)S(1)} collective-permute-done((bf16[256,1024]{1,0:T(8,128)(2,1)S(1)}, bf16[256,1024]{1,0:T(8,128)(2,1)S(1)}, u32[]{:S(2)}, u32[]{:S(2)}) %collective-permute-start.5) | collective-permute-done | bytes 524320 | tf_op jit(solution)/shard_map/ppermute | solution.py:293
  37.9 0.7 slice.51
  38.7 3.4 %collective-permute-start.7 = (bf16[128,1024]{1,0:T(8,128)(2,1)}, bf16[128,1024]{1,0:T(8,128)(2,1)S(1)}, u32[]{:S(2)}, u32[]{:S(2)}) collective-permute-start(bf16[128,1024]{1,0:T(8,128)(2,1)} %slice.51), channel_id=1, source_target_pairs={{0,3},{1,0},{2,1},{3,2},{4,7},{5,4},{6,5},{7,6},{8,11},{9,8},{10,9... | collective-permute-start | bytes 786440 | tf_op jit(solution)/shard_map/ppermute | solution.py:295
  42.1 0.8 slice.50
  42.9 2.3 %lists.1 = (s32[1,256]{1,0:T(1,128)}, s32[1,256]{1,0:T(1,128)}) custom-call(s32[1,4]{1,0:T(1,128)} %counts.1, s32[4,2,240]{2,1,0:T(2,128)} %bitcast.22, s32[32,32]{1,0:T(8,128)} %bitcast.18), custom_call_target="tpu_custom_call" | custom-call | tf_op jit(solution)/shard_map/lists/pallas_call | solution.py:110
  45.2 1.5 collective-permute-done.2.r2
  47.4 21.4 %own.1.before = f32[32,8,32,128]{3,2,1,0:T(8,128)} custom-call(s32[1024]{0:T(1024)} %anchors.3, s32[32,32]{1,0:T(8,128)} %bitcast.19, s32[1,256]{1,0:T(1,128)} %get-tuple-element.20.listed, bf16[256,1024]{1,0:T(8,128)(2,1)} %get-tuple-element.21.s, bf16[256,1024]{1,0:T(8,128)(2,1)} %copy-done.1, bf16[256,1024]{1,0:T(8,128)(2,1)} %copy-done, ...), custom_call_target="tpu_custom_call" | custom-call | tf_op jit(solution)/shard_map/own/pallas_call | solution.py:335
  69.6 25.8 %far.1 = (bf16[256,1024]{1,0:T(8,128)(2,1)}, bf16[256,1024]{1,0:T(8,128)(2,1)}, bf16[128,1024]{1,0:T(8,128)(2,1)}, bf16[128,1024]{1,0:T(8,128)(2,1)}, bf16[256,1...) custom-call(s32[1024]{0:T(1024)} %anchors.3, ...), custom_call_target="tpu_custom_call" | custom-call | tf_op jit(solution)/shard_map/far/pallas_call | solution.py:341
  95.3 1.4 collective-permute-start.14
  96.7 1.0 slice.41
  97.7 1.0 slice.42
  98.7 1.0 slice.45
  99.7 1.0 slice.46
  100.9 2.5 %collective-permute-start.10 = (bf16[128,1024]{1,0:T(8,128)(2,1)}, bf16[128,1024]{1,0:T(8,128)(2,1)S(1)}, u32[]{:S(2)}, u32[]{:S(2)}) collective-permute-start(bf16[128,1024]{1,0:T(8,128)(2,1)} %get-tuple-element.27), channel_id=1, source_target_pairs={{0,3},{1,0},{2,1},{3,2},{4,7},{5,4},{6,5},{7,6},{8,11},{9,8},{10,9... | collective-permute-start | bytes 786440 | tf_op jit(solution)/shard_map/ppermute | solution.py:304
  103.8 1.0 add_convert_fusion.1
  104.9 2.5 %collective-permute-start.15 = (bf16[256,1024]{1,0:T(8,128)(2,1)S(1)}, bf16[256,1024]{1,0:T(8,128)(2,1)S(1)}, u32[]{:S(2)}, u32[]{:S(2)}) collective-permute-start(bf16[256,1024]{1,0:T(8,128)(2,1)S(1)} %pad_maximum_fusion.3), channel_id=1, source_target_pairs={{0,3},{1,0},{2,1},{3,2},{4,7},{5,4},{6,5},{7,6},{8,11},{9,8},{10,9... | collective-permute-start | bytes 1572872 | tf_op jit(solution)/shard_map/ppermute | solution.py:311
  107.3 8.2 %collective-permute-done.12 = bf16[128,1024]{1,0:T(8,128)(2,1)S(1)} collective-permute-done((bf16[128,1024]{1,0:T(8,128)(2,1)}, bf16[128,1024]{1,0:T(8,128)(2,1)S(1)}, u32[]{:S(2)}, u32[]{:S(2)}) %collective-permute-start.12) | collective-permute-done | bytes 262176 | tf_op jit(solution)/shard_map/ppermute | solution.py:303
  115.6 1.0 add_convert_fusion.2
  117.0 2.7 %collective-permute-start.11 = (bf16[256,1024]{1,0:T(8,128)(2,1)S(1)}, bf16[256,1024]{1,0:T(8,128)(2,1)S(1)}, u32[]{:S(2)}, u32[]{:S(2)}) collective-permute-start(bf16[256,1024]{1,0:T(8,128)(2,1)S(1)} %pad_maximum_fusion.1), channel_id=1, source_target_pairs={{0,3},{1,0},{2,1},{3,2},{4,7},{5,4},{6,5},{7,6},{8,11},{9,8},{10,9... | collective-permute-start | bytes 1572872 | tf_op jit(solution)/shard_map/ppermute | solution.py:311
  120.3 10.3 %collective-permute-done.13 = bf16[256,1024]{1,0:T(8,128)(2,1)S(1)} collective-permute-done((bf16[256,1024]{1,0:T(8,128)(2,1)S(1)}, bf16[256,1024]{1,0:T(8,128)(2,1)S(1)}, u32[]{:S(2)}, u32[]{:S(2)}) %collective-permute-start.13) | collective-permute-done | bytes 524320 | tf_op jit(solution)/shard_map/ppermute | solution.py:311
  130.6 1.1 fusion
  131.7 10.2 %all-to-all-start.1 = ((bf16[32,8,1024]{2,1,0:T(8,128)(2,1)}), bf16[32,8,1024]{2,1,0:T(8,128)(2,1)S(1)}, u32[]{:S(2)}, u32[]{:S(2)}) async-start(bf16[32,8,1024]{2,1,0:T(8,128)(2,1)} %fusion), calls=%async_computation.1 | async-start | bytes 1048576 | tf_op jit(solution)/shard_map/all_to_all | solution.py:347
  142.0 11.4 %all-to-all-done.1 = bf16[32,8,1024]{2,1,0:T(8,128)(2,1)S(1)} async-done(((bf16[32,8,1024]{2,1,0:T(8,128)(2,1)}), bf16[32,8,1024]{2,1,0:T(8,128)(2,1)S(1)}, u32[]{:S(2)}, u32[]{:S(2)}) %all-to-all-start.1) | async-done | bytes 524320 | tf_op jit(solution)/shard_map/all_to_all | solution.py:347
  153.3 0.8 copy-done.3
  154.1 5.1 %finish.1 = f32[256,1024]{1,0:T(8,128)} custom-call(s32[32,32]{1,0:T(8,128)} %bitcast.21, bf16[256,1024]{1,0:T(8,128)(2,1)} %get-tuple-element.23.p0, bf16[256,1024]{1,0:T(8,128)(2,1)} %copy-done.12, bf16[256,1024]{1,0:T(8,128)(2,1)} %copy-done.11, bf16[256,1024]{1,0:T(8,128)(2,1)} %bitcast.14), custom_call_target="tpu_custom_call" | custom-call | tf_op jit(solution)/shard_map/finish/pallas_call | solution.py:348
  (56 shorter events, 3.1 us)
Async XLA Ops:
  3.3 20.9 %all-to-all-start = ((bf16[32,8,1024]{2,1,0:T(8,128)(2,1)}), bf16[32,8,1024]{2,1,0:T(8,128)(2,1)S(1)}, u32[]{:S(2)}, u32[]{:S(2)}) async-start(bf16[32,8,1024]{2,1,0:T(8,128)(2,1)} %bitcast.16), calls=%async_computation | async-start | bytes 1048576 | tf_op jit(solution)/shard_map/all_to_all | solution.py:323
  12.7 14.2 %collective-permute-start.1 = (bf16[256,1024]{1,0:T(8,128)(2,1)}, bf16[256,1024]{1,0:T(8,128)(2,1)S(1)}, u32[]{:S(2)}, u32[]{:S(2)}) collective-permute-start(bf16[256,1024]{1,0:T(8,128)(2,1)} %get-tuple-element.21.s), channel_id=1, source_target_pairs={{0,3},{1,0},{2,1},{3,2},{4,7},{5,4},{6,5},{7,6},{8,11},{9,8},{10,9... | collective-permute-start | bytes 1572872 | tf_op jit(solution)/shard_map/ppermute | solution.py:293
  15.5 14.8 %collective-permute-start = (bf16[256,1024]{1,0:T(8,128)(2,1)}, bf16[256,1024]{1,0:T(8,128)(2,1)S(1)}, u32[]{:S(2)}, u32[]{:S(2)}) collective-permute-start(bf16[256,1024]{1,0:T(8,128)(2,1)} %get-tuple-element.21.s), channel_id=1, source_target_pairs={{0,1},{1,2},{2,3},{3,0},{4,5},{5,6},{6,7},{7,4},{8,9},{9,10},{10,1... | collective-permute-start | bytes 1572872 | tf_op jit(solution)/shard_map/ppermute | solution.py:292
  24.1 44.6 %copy-start.2 = (bf16[32,8,1024]{2,1,0:T(8,128)(2,1)}, bf16[32,8,1024]{2,1,0:T(8,128)(2,1)S(1)}, u32[]{:S(2)}) copy-start(bf16[32,8,1024]{2,1,0:T(8,128)(2,1)S(1)} %all-to-all-done) | copy-start | bytes 1572868
  24.1 13.8 %collective-permute-start.5 = (bf16[256,1024]{1,0:T(8,128)(2,1)S(1)}, bf16[256,1024]{1,0:T(8,128)(2,1)S(1)}, u32[]{:S(2)}, u32[]{:S(2)}) collective-permute-start(bf16[256,1024]{1,0:T(8,128)(2,1)S(1)} %bitcast.11), channel_id=1, source_target_pairs={{0,3},{1,0},{2,1},{3,2},{4,7},{5,4},{6,5},{7,6},{8,11},{9,8},{10,9... | collective-permute-start | bytes 1572872 | tf_op jit(solution)/shard_map/ppermute | solution.py:293
  26.9 15.2 %collective-permute-start.4 = (bf16[256,1024]{1,0:T(8,128)(2,1)S(1)}, bf16[256,1024]{1,0:T(8,128)(2,1)S(1)}, u32[]{:S(2)}, u32[]{:S(2)}) collective-permute-start(bf16[256,1024]{1,0:T(8,128)(2,1)S(1)} %bitcast.12), channel_id=1, source_target_pairs={{0,1},{1,2},{2,3},{3,0},{4,5},{5,6},{6,7},{7,4},{8,9},{9,10},{10,1... | collective-permute-start | bytes 1572872 | tf_op jit(solution)/shard_map/ppermute | solution.py:292
  26.9 19.8 %copy-start = (bf16[256,1024]{1,0:T(8,128)(2,1)}, bf16[256,1024]{1,0:T(8,128)(2,1)S(1)}, u32[]{:S(2)}) copy-start(bf16[256,1024]{1,0:T(8,128)(2,1)S(1)} %collective-permute-done.1.l) | copy-start | bytes 1572868
  26.9 18.3 %collective-permute-start.3 = (bf16[128,1024]{1,0:T(8,128)(2,1)S(1)}, bf16[128,1024]{1,0:T(8,128)(2,1)S(1)}, u32[]{:S(2)}, u32[]{:S(2)}) collective-permute-start(bf16[128,1024]{1,0:T(8,128)(2,1)S(1)} %slice.49), channel_id=1, source_target_pairs={{0,3},{1,0},{2,1},{3,2},{4,7},{5,4},{6,5},{7,6},{8,11},{9,8},{10,9... | collective-permute-start | bytes 786440 | tf_op jit(solution)/shard_map/ppermute | solution.py:295
  30.3 16.4 %copy-start.1 = (bf16[256,1024]{1,0:T(8,128)(2,1)}, bf16[256,1024]{1,0:T(8,128)(2,1)S(1)}, u32[]{:S(2)}) copy-start(bf16[256,1024]{1,0:T(8,128)(2,1)S(1)} %collective-permute-done.r) | copy-start | bytes 1572868
  31.0 15.6 %collective-permute-start.2 = (bf16[128,1024]{1,0:T(8,128)(2,1)}, bf16[128,1024]{1,0:T(8,128)(2,1)S(1)}, u32[]{:S(2)}, u32[]{:S(2)}) collective-permute-start(bf16[128,1024]{1,0:T(8,128)(2,1)} %slice.48), channel_id=1, source_target_pairs={{0,1},{1,2},{2,3},{3,0},{4,5},{5,6},{6,7},{7,4},{8,9},{9,10},{10,1... | collective-permute-start | bytes 786440 | tf_op jit(solution)/shard_map/ppermute | solution.py:294
  37.9 30.9 %copy-start.4 = (bf16[256,1024]{1,0:T(8,128)(2,1)}, bf16[256,1024]{1,0:T(8,128)(2,1)S(1)}, u32[]{:S(2)}) copy-start(bf16[256,1024]{1,0:T(8,128)(2,1)S(1)} %collective-permute-done.5.fl) | copy-start | bytes 1572868
  38.7 30.1 %collective-permute-start.7 = (bf16[128,1024]{1,0:T(8,128)(2,1)}, bf16[128,1024]{1,0:T(8,128)(2,1)S(1)}, u32[]{:S(2)}, u32[]{:S(2)}) collective-permute-start(bf16[128,1024]{1,0:T(8,128)(2,1)} %slice.51), channel_id=1, source_target_pairs={{0,3},{1,0},{2,1},{3,2},{4,7},{5,4},{6,5},{7,6},{8,11},{9,8},{10,9... | collective-permute-start | bytes 786440 | tf_op jit(solution)/shard_map/ppermute | solution.py:295
  42.1 26.7 %copy-start.5 = (bf16[256,1024]{1,0:T(8,128)(2,1)}, bf16[256,1024]{1,0:T(8,128)(2,1)S(1)}, u32[]{:S(2)}) copy-start(bf16[256,1024]{1,0:T(8,128)(2,1)S(1)} %collective-permute-done.4.fr) | copy-start | bytes 1572868
  42.9 25.9 %collective-permute-start.6 = (bf16[128,1024]{1,0:T(8,128)(2,1)}, bf16[128,1024]{1,0:T(8,128)(2,1)S(1)}, u32[]{:S(2)}, u32[]{:S(2)}) collective-permute-start(bf16[128,1024]{1,0:T(8,128)(2,1)} %slice.50), channel_id=1, source_target_pairs={{0,1},{1,2},{2,3},{3,0},{4,5},{5,6},{6,7},{7,4},{8,9},{9,10},{10,1... | collective-permute-start | bytes 786440 | tf_op jit(solution)/shard_map/ppermute | solution.py:294
  45.2 1.5 copy-start.6
  68.8 0.7 copy-start.13
  68.8 0.8 copy-start.14
  95.3 21.6 %copy-start.9 = (bf16[256,1024]{1,0:T(8,128)(2,1)S(1)}, bf16[256,1024]{1,0:T(8,128)(2,1)}, u32[]{:S(2)}) copy-start(bf16[256,1024]{1,0:T(8,128)(2,1)} %get-tuple-element.26) | copy-start | bytes 1572868
  95.3 24.4 %copy-start.8 = (bf16[256,1024]{1,0:T(8,128)(2,1)S(1)}, bf16[256,1024]{1,0:T(8,128)(2,1)}, u32[]{:S(2)}) copy-start(bf16[256,1024]{1,0:T(8,128)(2,1)} %get-tuple-element.24) | copy-start | bytes 1572868
  95.3 8.5 %collective-permute-start.14 = (bf16[128,1024]{1,0:T(8,128)(2,1)}, bf16[128,1024]{1,0:T(8,128)(2,1)S(1)}, u32[]{:S(2)}, u32[]{:S(2)}) collective-permute-start(bf16[128,1024]{1,0:T(8,128)(2,1)} %get-tuple-element.32), channel_id=1, source_target_pairs={{0,3},{1,0},{2,1},{3,2},{4,7},{5,4},{6,5},{7,6},{8,11},{9,8},{10,9... | collective-permute-start | bytes 786440 | tf_op jit(solution)/shard_map/ppermute | solution.py:304
  98.7 31.9 %copy-start.10 = (bf16[256,1024]{1,0:T(8,128)(2,1)S(1)}, bf16[256,1024]{1,0:T(8,128)(2,1)}, u32[]{:S(2)}) copy-start(bf16[256,1024]{1,0:T(8,128)(2,1)} %get-tuple-element.28) | copy-start | bytes 1572868
  100.7 19.1 %collective-permute-start.8 = (bf16[128,1024]{1,0:T(8,128)(2,1)}, bf16[128,1024]{1,0:T(8,128)(2,1)S(1)}, u32[]{:S(2)}, u32[]{:S(2)}) collective-permute-start(bf16[128,1024]{1,0:T(8,128)(2,1)} %get-tuple-element.25), channel_id=1, source_target_pairs={{0,1},{1,2},{2,3},{3,0},{4,5},{5,6},{6,7},{7,4},{8,9},{9,10},{10,1... | collective-permute-start | bytes 786440 | tf_op jit(solution)/shard_map/ppermute | solution.py:303
  100.9 16.0 %collective-permute-start.10 = (bf16[128,1024]{1,0:T(8,128)(2,1)}, bf16[128,1024]{1,0:T(8,128)(2,1)S(1)}, u32[]{:S(2)}, u32[]{:S(2)}) collective-permute-start(bf16[128,1024]{1,0:T(8,128)(2,1)} %get-tuple-element.27), channel_id=1, source_target_pairs={{0,3},{1,0},{2,1},{3,2},{4,7},{5,4},{6,5},{7,6},{8,11},{9,8},{10,9... | collective-permute-start | bytes 786440 | tf_op jit(solution)/shard_map/ppermute | solution.py:304
  103.4 12.1 %collective-permute-start.12 = (bf16[128,1024]{1,0:T(8,128)(2,1)}, bf16[128,1024]{1,0:T(8,128)(2,1)S(1)}, u32[]{:S(2)}, u32[]{:S(2)}) collective-permute-start(bf16[128,1024]{1,0:T(8,128)(2,1)} %get-tuple-element.30), channel_id=1, source_target_pairs={{0,1},{1,2},{2,3},{3,0},{4,5},{5,6},{6,7},{7,4},{8,9},{9,10},{10,1... | collective-permute-start | bytes 786440 | tf_op jit(solution)/shard_map/ppermute | solution.py:303
  104.9 15.4 %collective-permute-start.15 = (bf16[256,1024]{1,0:T(8,128)(2,1)S(1)}, bf16[256,1024]{1,0:T(8,128)(2,1)S(1)}, u32[]{:S(2)}, u32[]{:S(2)}) collective-permute-start(bf16[256,1024]{1,0:T(8,128)(2,1)S(1)} %pad_maximum_fusion.3), channel_id=1, source_target_pairs={{0,3},{1,0},{2,1},{3,2},{4,7},{5,4},{6,5},{7,6},{8,11},{9,8},{10,9... | collective-permute-start | bytes 1572872 | tf_op jit(solution)/shard_map/ppermute | solution.py:311
  116.6 14.0 %collective-permute-start.13 = (bf16[256,1024]{1,0:T(8,128)(2,1)S(1)}, bf16[256,1024]{1,0:T(8,128)(2,1)S(1)}, u32[]{:S(2)}, u32[]{:S(2)}) collective-permute-start(bf16[256,1024]{1,0:T(8,128)(2,1)S(1)} %pad_maximum_fusion.2), channel_id=1, source_target_pairs={{0,1},{1,2},{2,3},{3,0},{4,5},{5,6},{6,7},{7,4},{8,9},{9,10},{10,1... | collective-permute-start | bytes 1572872 | tf_op jit(solution)/shard_map/ppermute | solution.py:311
  117.0 24.9 %collective-permute-start.11 = (bf16[256,1024]{1,0:T(8,128)(2,1)S(1)}, bf16[256,1024]{1,0:T(8,128)(2,1)S(1)}, u32[]{:S(2)}, u32[]{:S(2)}) collective-permute-start(bf16[256,1024]{1,0:T(8,128)(2,1)S(1)} %pad_maximum_fusion.1), channel_id=1, source_target_pairs={{0,3},{1,0},{2,1},{3,2},{4,7},{5,4},{6,5},{7,6},{8,11},{9,8},{10,9... | collective-permute-start | bytes 1572872 | tf_op jit(solution)/shard_map/ppermute | solution.py:311
  119.9 22.1 %collective-permute-start.9 = (bf16[256,1024]{1,0:T(8,128)(2,1)S(1)}, bf16[256,1024]{1,0:T(8,128)(2,1)S(1)}, u32[]{:S(2)}, u32[]{:S(2)}) collective-permute-start(bf16[256,1024]{1,0:T(8,128)(2,1)S(1)} %pad_maximum_fusion), channel_id=1, source_target_pairs={{0,1},{1,2},{2,3},{3,0},{4,5},{5,6},{6,7},{7,4},{8,9},{9,10},{10,1... | collective-permute-start | bytes 1572872 | tf_op jit(solution)/shard_map/ppermute | solution.py:311
  131.7 21.7 %all-to-all-start.1 = ((bf16[32,8,1024]{2,1,0:T(8,128)(2,1)}), bf16[32,8,1024]{2,1,0:T(8,128)(2,1)S(1)}, u32[]{:S(2)}, u32[]{:S(2)}) async-start(bf16[32,8,1024]{2,1,0:T(8,128)(2,1)} %fusion), calls=%async_computation.1 | async-start | bytes 1048576 | tf_op jit(solution)/shard_map/all_to_all | solution.py:347
  141.9 11.4 %copy-start.11 = (bf16[256,1024]{1,0:T(8,128)(2,1)}, bf16[256,1024]{1,0:T(8,128)(2,1)S(1)}, u32[]{:S(2)}) copy-start(bf16[256,1024]{1,0:T(8,128)(2,1)S(1)} %collective-permute-done.11.p2) | copy-start | bytes 1572868
  141.9 11.4 %copy-start.12 = (bf16[256,1024]{1,0:T(8,128)(2,1)}, bf16[256,1024]{1,0:T(8,128)(2,1)S(1)}, u32[]{:S(2)}) copy-start(bf16[256,1024]{1,0:T(8,128)(2,1)S(1)} %collective-permute-done.9.p1) | copy-start | bytes 1572868
  153.3 0.8 copy-start.3
  (1 other events, 0.7 us)

commit v3 on v2

--- a/solution.py
+++ b/solution.py
@@ -134,11 +134,15 @@
     unpack_slab(far_high, 128, boxes, base + 16, (position + 2) & 3)
 
 
-def run_pairs(base, anchors, wanted, listed, boxes, sums, blocks, along_x, inverse, density, field):
+def run_pairs(base, anchors, wanted, listed, boxes, sums, blocks, along_x, inverse, work):
+    density, one, two, three, field = work
+    first, second = sums
     member = lax.axis_index("orb")
-    count = listed[0, LIST - 1]
-
-    def fields(entry):
+    batches = (listed[0, LIST - 1] + BATCH - 1) // BATCH
+    field[...] = jnp.zeros_like(field)
+
+    def fields(k):
+        entry = listed[0, k]
         i = entry & 31
         c = (entry >> 5) & 31
         if base:
@@ -146,103 +150,146 @@
         else:
             other = member * 32 + c
         shifted = MARGIN + anchors[member * 32 + i] - anchors[other]
-        return (i, base + c, shifted, entry >> 11)
+        return (i, c, shifted, (entry >> 11).astype(F32))
+
+    def part(p, h):
+        return (slice(p * EXT, (p + 1) * EXT), slice(h * 128, (h + 1) * 128))
+
+    def quads(a, b, c, d):
+        s1, s2, s3, s4 = a + b, a - b, c + d, c - d
+        return (s1 + s3, s2 + s4, s1 - s3, s2 - s4)
+
+    def product(b, p):
+        i, c, shifted, _ = fields(b * BATCH + p)
+        for h in range(2):
+            f = [
+                boxes[i, 2 * q + h, pl.ds(MARGIN, EXT), :] * boxes[base + c, 2 * q + h, pl.ds(shifted, EXT), :]
+                for q in range(4)
+            ]
+            rows, lanes = part(p, h)
+            for q, v in enumerate(quads(*f)):
+                density[q, rows, lanes] = v.astype(BF16)
+
+    def terms(b, p):
+        i, c, shifted, weight = fields(b * BATCH + p)
+        for h in range(2):
+            rows, lanes = part(p, h)
+            v = [u * weight for u in quads(*(field[q, rows, lanes] for q in range(4)))]
+            for q in range(4):
+                first[i, 2 * q + h] += v[q] * boxes[base + c, 2 * q + h, pl.ds(shifted, EXT), :]
+            for q in range(4):
+                second[c, 2 * q + h, pl.ds(shifted, EXT), :] += v[q] * boxes[i, 2 * q + h, pl.ds(MARGIN, EXT), :]
+
+    def step(stage, q):
+        if stage == 0:
+            one[q] = jnp.dot(density[q], blocks[q], preferred_element_type=F32).astype(BF16)
+        elif stage == 1:
+            t = jnp.dot(along_x[...], one[q], preferred_element_type=F32)
+            two[q] = (t.reshape(BATCH, EXT, 256) * inverse[q][None]).reshape(BATCH * EXT, 256).astype(BF16)
+        elif stage == 2:
+            three[q] = jnp.dot(along_x[...], two[q], preferred_element_type=F32).astype(BF16)
+        else:
+            field[q] = lax.dot_general(three[q], blocks[q], (((1,), (1,)), ((), ())), preferred_element_type=F32)
 
     def batch(b, carry):
-        for p in range(BATCH):
-            i, j, shifted, weight = fields(listed[0, b * BATCH + p])
-            for h in range(2):
-                f = []
-                for q in range(4):
-                    c = 2 * q + h
-                    f.append(boxes[i, c, pl.ds(MARGIN, EXT), :] * boxes[j, c, pl.ds(shifted, EXT), :])
-                a, bb, cc, d = f
-                s1, s2, s3, s4 = a + bb, a - bb, cc + d, cc - d
-                for q, v in enumerate((s1 + s3, s2 + s4, s1 - s3, s2 - s4)):
-                    density[q, p * EXT : (p + 1) * EXT, h * 128 : (h + 1) * 128] = v.astype(BF16)
-        for q in range(4):
-            t = jnp.dot(density[q], blocks[q], preferred_element_type=F32).astype(BF16)
-            t = jnp.dot(along_x[...], t, preferred_element_type=F32)
-            t = (t.reshape(BATCH, EXT, 256) * inverse[q][None]).reshape(BATCH * EXT, 256).astype(BF16)
-            t = jnp.dot(along_x[...], t, preferred_element_type=F32).astype(BF16)
-            field[q] = lax.dot_general(t, blocks[q], (((1,), (1,)), ((), ())), preferred_element_type=F32)
-        for p in range(BATCH):
-            i, j, shifted, weight = fields(listed[0, b * BATCH + p])
-            scale = weight.astype(F32)
-            for h in range(2):
-                ee, eo, oe, oo = (
-                    field[q, p * EXT : (p + 1) * EXT, h * 128 : (h + 1) * 128] for q in range(4)
-                )
-                s1, s2, s3, s4 = ee + eo, ee - eo, oe + oo, oe - oo
-                for q, v in enumerate((s1 + s3, s2 + s4, s1 - s3, s2 - s4)):
-                    c = 2 * q + h
-                    v = v * scale
-                    sums[i, c, pl.ds(MARGIN, EXT), :] += v * boxes[j, c, pl.ds(shifted, EXT), :]
-                    sums[j, c, pl.ds(shifted, EXT), :] += v * boxes[i, c, pl.ds(MARGIN, EXT), :]
+        for k in range(8):
+            step(k // 4, k % 4)
+            terms(jnp.maximum(b - 1, 0), k)
+        for k in range(8):
+            step(2 + k // 4, k % 4)
+            product(b + 1, k)
         return carry
 
-    lax.fori_loop(0, (count + BATCH - 1) // BATCH, batch, 0)
-
-
-def clear_rows(ref, first, last):
-    def one(k, carry):
-        ref[pl.ds(first + k, 1)] = jnp.zeros((1,) + ref.shape[1:], F32)
+    for p in range(BATCH):
+        product(0, p)
+    lax.fori_loop(0, batches, batch, 0)
+    for p in range(BATCH):
+        terms(jnp.maximum(batches - 1, 0), p)
+
+
+def prepare(boxes, sums):
+    first, second = sums
+
+    def margins(k, carry):
+        for c in range(CHUNKS):
+            boxes[k, c, 0:MARGIN, :] = jnp.zeros((MARGIN, 128), F32)
+            boxes[k, c, MARGIN + EXT : PAD, :] = jnp.zeros((MARGIN, 128), F32)
         return carry
 
-    lax.fori_loop(0, last - first, one, 0)
-
-
-def own_kernel(anchors, wanted, listed, s, r, l, r2, l2, blocks, along_x, inverse, out, boxes, sums, density, field):
-    clear_rows(boxes, 0, 32)
-    clear_rows(sums, 0, 32)
-    fill((s, r, l, r2, l2), boxes, 0)
-    run_pairs(0, anchors, wanted, listed, boxes, sums, blocks, along_x, inverse, density, field)
-
-    def one(k, carry):
-        for c in range(CHUNKS):
-            out[pl.ds(k, 1), c] = sums[pl.ds(k, 1), c, MARGIN : MARGIN + EXT, :]
+    lax.fori_loop(0, boxes.shape[0], margins, 0)
+
+    def blank(k, carry):
+        first[pl.ds(k, 1)] = jnp.zeros((1, CHUNKS, EXT, 128), F32)
+        second[pl.ds(k, 1)] = jnp.zeros((1, CHUNKS, PAD, 128), F32)
         return carry
 
-    lax.fori_loop(0, 32, one, 0)
-
-
-def pack_sums(sums, base, outs):
+    lax.fori_loop(0, 32, blank, 0)
+
+
+def pack_sums(outs, terms):
     position = lax.axis_index("grp")
-    own, ahead, low, high, behind = outs
+    own, ahead, low, high, behind = range(5)
     for step, first, target in ((2, 0, low), (2, 16, high), (1, 0, ahead), (3, 0, behind), (0, 0, own)):
-        start = pl.multiple_of(MARGIN + 8 * ((position + step) & 3), 8)
+        start = 8 * ((position + step) & 3)
 
         def one(k, carry):
             for c in range(CHUNKS):
-                part = sums[pl.ds(base + first + 2 * k, 2), c, pl.ds(start, 8), :].reshape(16, 128)
-                target[pl.ds(k * 16, 16), c * 128 : (c + 1) * 128] = part.astype(BF16)
+                value = None
+                for ref, margin in terms:
+                    rows = pl.ds(pl.multiple_of(start + margin, 8), 8)
+                    term = ref[pl.ds(first + 2 * k, 2), c, rows, :].reshape(16, 128)
+                    value = term if value is None else value + term
+                outs[target][pl.ds(pl.multiple_of(k * 16, 16), 16), c * 128 : (c + 1) * 128] = value.astype(BF16)
             return carry
 
-        lax.fori_loop(0, target.shape[0] // 16, one, 0)
-
-
-def far_kernel(
-    anchors, wanted, listed, before,
-    s, r, l, r2, l2,
-    fs, fr, fl, fr2, fl2,
-    blocks, along_x, inverse,
-    o0, o1, o2, o3, o4, f0, f1, f2, f3, f4,
-    boxes, sums, density, field,
-):
-    clear_rows(boxes, 0, 64)
-    clear_rows(sums, 32, 64)
+        lax.fori_loop(0, outs[target].shape[0] // 16, one, 0)
+
+
+def unpack_sums(ins, ref):
+    position = lax.axis_index("grp")
+    own, ahead, low, high, behind = ins
+    for step, first, source in ((2, 0, low), (2, 16, high), (1, 0, ahead), (3, 0, behind), (0, 0, own)):
+        start = pl.multiple_of(8 * ((position + step) & 3), 8)
+
+        def one(k, carry):
+            for c in range(CHUNKS):
+                part = source[pl.ds(pl.multiple_of(k * 16, 16), 16), c * 128 : (c + 1) * 128].astype(F32)
+                ref[pl.ds(first + 2 * k, 2), c, pl.ds(start, 8), :] = part.reshape(2, 8, 128)
+            return carry
+
+        lax.fori_loop(0, source.shape[0] // 16, one, 0)
+
+
+def own_kernel(anchors, wanted, listed, s, r, l, r2, l2, blocks, along_x, inverse, *rest):
+    outs, boxes, sums, work = rest[:5], rest[5], rest[6:8], rest[8:]
+    prepare(boxes, sums)
     fill((s, r, l, r2, l2), boxes, 0)
-    fill((fs, fr, fl, fr2, fl2), boxes, 32)
-
-    def one(k, carry):
-        for c in range(CHUNKS):
-            sums[pl.ds(k, 1), c, MARGIN : MARGIN + EXT, :] = before[pl.ds(k, 1), c]
-        return carry
-
-    lax.fori_loop(0, 32, one, 0)
-    run_pairs(32, anchors, wanted, listed, boxes, sums, blocks, along_x, inverse, density, field)
-    pack_sums(sums, 32, (f0, f1, f2, f3, f4))
-    pack_sums(sums, 0, (o0, o1, o2, o3, o4))
+    run_pairs(0, anchors, wanted, listed, boxes, sums, blocks, along_x, inverse, work)
+    pack_sums(outs, ((sums[0], 0), (sums[1], MARGIN)))
+
+
+def far_kernel(anchors, wanted, listed, *rest):
+    before, own, far = rest[:5], rest[5:10], rest[10:15]
+    blocks, along_x, inverse = rest[15:18]
+    own_outs, far_outs, boxes, sums, work = rest[18:23], rest[23:28], rest[28], rest[29:31], rest[31:]
+    prepare(boxes, sums)
+    fill(own, boxes, 0)
+    fill(far, boxes, 32)
+    unpack_sums(before, sums[0])
+    run_pairs(32, anchors, wanted, listed, boxes, sums, blocks, along_x, inverse, work)
+    pack_sums(far_outs, ((sums[1], MARGIN),))
+    pack_sums(own_outs, ((sums[0], 0),))
+
+
+def scratch(total):
+    stage = pltpu.VMEM((4, BATCH * EXT, 256), BF16)
+    return [
+        pltpu.VMEM((total, CHUNKS, PAD, 128), F32),
+        pltpu.VMEM((32, CHUNKS, EXT, 128), F32),
+        pltpu.VMEM((32, CHUNKS, PAD, 128), F32),
+        stage, stage, stage, stage,
+        pltpu.VMEM((4, BATCH * EXT, 256), F32),
+    ]
 
 
 def finish_kernel(wanted, p0, p1, p2, returned, out, matrix, total):
@@ -274,6 +321,11 @@
 VMEM = pl.BlockSpec(memory_space=pltpu.VMEM)
 
 
+SLAB = jax.ShapeDtypeStruct((256, PLANE), BF16)
+HALF_SLAB = jax.ShapeDtypeStruct((128, PLANE), BF16)
+PARTS = [(VMEM, shape) for shape in (SLAB, SLAB, HALF_SLAB, HALF_SLAB, SLAB)]
+
+
 def call(kernel, name, ins, outs, scratch):
     return pl.pallas_call(
         kernel,
@@ -314,9 +366,8 @@
 def shards(orbitals, anchors, wanted, pairs, counts):
     blocks, along_x, inverse = (jnp.asarray(t) for t in tables())
     wanted = wanted.reshape(32, 32)
-    slab_type = jax.ShapeDtypeStruct((256, PLANE), BF16)
     slab, outgoing = call(
-        order_kernel, "order", [SMEM, VMEM], [(VMEM, slab_type)] * 2,
+        order_kernel, "order", [SMEM, VMEM], [(VMEM, SLAB)] * 2,
         [pltpu.VMEM((PLANE, PLANE), BF16), pltpu.VMEM((256, PLANE), F32)],
     )(wanted, orbitals.reshape(256, PLANE))
     own = ring(slab)
@@ -324,23 +375,13 @@
     own_list, far_list = make_lists(counts, pairs, wanted)
     far = ring(incoming)
 
-    def work(total):
-        return [
-            pltpu.VMEM((total, CHUNKS, PAD, 128), F32),
-            pltpu.VMEM((total, CHUNKS, PAD, 128), F32),
-            pltpu.VMEM((4, BATCH * EXT, 256), BF16),
-            pltpu.VMEM((4, BATCH * EXT, 256), F32),
-        ]
-
-    (before,) = call(
-        own_kernel, "own", [SMEM] * 3 + [VMEM] * 8,
-        [(VMEM, jax.ShapeDtypeStruct((32, CHUNKS, EXT, 128), F32))], work(32),
-    )(anchors, wanted, own_list, *own, blocks, along_x, inverse)
-    half_type = jax.ShapeDtypeStruct((128, PLANE), BF16)
-    packed = [(VMEM, t) for t in (slab_type, slab_type, half_type, half_type, slab_type)]
-    parts = call(
-        far_kernel, "far", [SMEM] * 3 + [VMEM] * 14, packed * 2, work(64),
-    )(anchors, wanted, far_list, before, *own, *far, blocks, along_x, inverse)
+    tables_in = (blocks, along_x, inverse)
+    before = call(own_kernel, "own", [SMEM] * 3 + [VMEM] * 8, PARTS, scratch(32))(
+        anchors, wanted, own_list, *own, *tables_in
+    )
+    parts = call(far_kernel, "far", [SMEM] * 3 + [VMEM] * 18, PARTS * 2, scratch(64))(
+        anchors, wanted, far_list, *before, *own, *far, *tables_in
+    )
     far_got = scatter(parts[5:])
     own_got = scatter(parts[:5])
     far_sum = sum(part.astype(F32) for part in far_got).astype(BF16)

time: 160 us -> 142 us (0.89)
  Pallas kernels: 57.9 us -> 44.1 us
  local copies, waits for them, and re-layouts: 8.5 us -> 5.43 us
  other arithmetic: 3.37 us -> 1.47 us
    pallas_call x3, Pallas kernels: 50.4 us -> 36.6 us  [the longest x1 18 us: shards(): call(far_kernel, 'far', [SMEM] * 3 + [VMEM] * 18, PARTS * 2, scratch(64))]
    ppermute x2, waiting for transfers between devices: 10.3 us -> 5.59 us  [scatter(): lax.ppermute(ahead, 'grp', up)]
    ppermute x2, waiting for transfers between devices: 0.35 us -> 3.72 us  [scatter(): lax.ppermute(behind, 'grp', down)]
    all_to_all x1, starting transfers between devices: 10.2 us -> 12.3 us  [shards(): lax.all_to_all(far_sum, 'orb', split_axis=0, concat_axis=0, tiled=True)]
    unnamed x30 -> x40, local copies, waits for them, and re-layouts: 2.26 us -> 4.28 us
    slice x2, local copies, waits for them, and re-layouts: 1.94 us -> 0.04 us  [scatter(): behind = jnp.concatenate([behind[:128], add(behind[128:], high)], axis=0)]
    convert_element_type x4, other arithmetic: 2.16 us -> 0.27 us  [add(): return (a.astype(F32) + b.astype(F32)).astype(BF16)]
    ppermute x2, starting transfers between devices: 3.92 us -> 2.11 us  [scatter(): high = lax.ppermute(high, 'grp', down)]
  transfers between devices with their start and end apart: 18 -> 18, of which waited for: 8 -> 8; matrix products, arithmetic and copies ran while one was open for 6% -> 2% of each run, Pallas kernels for 15% -> 12%
where the time goes in v3:
time: 142 us
  waiting for transfers between devices  48.1 us (34%)
  Pallas kernels  44.1 us (31%)
  starting transfers between devices  42.5 us (30%)
  local copies, waits for them, and re-layouts  5.43 us (4%)
  other arithmetic  1.47 us (1%)
    pallas_call x1, Pallas kernels, shards(): call(far_kernel, 'far', [SMEM] * 3 + [VMEM] * 18, PARTS * 2, scratch(64))  18 us
    pallas_call x1, Pallas kernels, shards(): call(own_kernel, 'own', [SMEM] * 3 + [VMEM] * 8, PARTS, scratch(32))  15.4 us
    all_to_all x1, starting transfers between devices, shards(): lax.all_to_all(far_sum, 'orb', split_axis=0, concat_axis=0, tiled=True)  12.3 us
    all_to_all x1, waiting for transfers between devices, shards(): lax.all_to_all(far_sum, 'orb', split_axis=0, concat_axis=0, tiled=True)  11.4 us
    all_to_all x1, starting transfers between devices, shards(): lax.all_to_all(outgoing, 'orb', split_axis=0, concat_axis=0, tiled=True)  9.55 us
    all_to_all x1, waiting for transfers between devices, shards(): lax.all_to_all(outgoing, 'orb', split_axis=0, concat_axis=0, tiled=True)  8.62 us
    ppermute x2, waiting for transfers between devices, scatter(): low = lax.ppermute(low, 'grp', up)  7.89 us
    ppermute x2, waiting for transfers between devices, ring(): right = lax.ppermute(slab, 'grp', down)  7.57 us
  transfers between devices with their start and end apart: 18, of which 8 were waited for; matrix products, arithmetic and copies ran while one was open for 2% of the time, Pallas kernels for 12%

profile of v3, /device:TPU:1, one launch (start us, length us, event | category | flops | bytes accessed | tf_op | source)
XLA Modules:
  0.0 142.0 jit_solution(9345741896210555342)
XLA Ops:
  0.0 3.3 %order.1 = (bf16[256,1024]{1,0:T(8,128)(2,1)}, bf16[256,1024]{1,0:T(8,128)(2,1)}) custom-call(s32[32,32]{1,0:T(8,128)} %bitcast.17, f32[256,1024]{1,0:T(8,128)} %bitcast.15), custom_call_target="tpu_custom_call" | custom-call | tf_op jit(solution)/shard_map/order/pallas_call | solution.py:369
  3.3 9.6 %all-to-all-start = ((bf16[32,8,1024]{2,1,0:T(8,128)(2,1)}), bf16[32,8,1024]{2,1,0:T(8,128)(2,1)S(1)}, u32[]{:S(2)}, u32[]{:S(2)}) async-start(bf16[32,8,1024]{2,1,0:T(8,128)(2,1)} %bitcast.16), calls=%async_computation | async-start | bytes 1048576 | tf_op jit(solution)/shard_map/all_to_all | solution.py:374
  12.8 2.8 %collective-permute-start.1 = (bf16[256,1024]{1,0:T(8,128)(2,1)S(1)}, bf16[256,1024]{1,0:T(8,128)(2,1)S(1)}, u32[]{:S(2)}, u32[]{:S(2)}) collective-permute-start(bf16[256,1024]{1,0:T(8,128)(2,1)S(1)} %copy-done.3), channel_id=1, source_target_pairs={{0,3},{1,0},{2,1},{3,2},{4,7},{5,4},{6,5},{7,6},{8,11},{9,8},{10,9... | collective-permute-start | bytes 1572872 | tf_op jit(solution)/shard_map/ppermute | solution.py:345
  15.6 8.6 %all-to-all-done = bf16[32,8,1024]{2,1,0:T(8,128)(2,1)S(1)} async-done(((bf16[32,8,1024]{2,1,0:T(8,128)(2,1)}), bf16[32,8,1024]{2,1,0:T(8,128)(2,1)S(1)}, u32[]{:S(2)}, u32[]{:S(2)}) %all-to-all-start) | async-done | bytes 524320 | tf_op jit(solution)/shard_map/all_to_all | solution.py:374
  24.3 2.7 %collective-permute-start.5 = (bf16[256,1024]{1,0:T(8,128)(2,1)S(1)}, bf16[256,1024]{1,0:T(8,128)(2,1)S(1)}, u32[]{:S(2)}, u32[]{:S(2)}) collective-permute-start(bf16[256,1024]{1,0:T(8,128)(2,1)S(1)} %bitcast.11), channel_id=1, source_target_pairs={{0,3},{1,0},{2,1},{3,2},{4,7},{5,4},{6,5},{7,6},{8,11},{9,8},{10,9... | collective-permute-start | bytes 1572872 | tf_op jit(solution)/shard_map/ppermute | solution.py:345
  27.0 3.2 %collective-permute-start.3 = (bf16[128,1024]{1,0:T(8,128)(2,1)S(1)}, bf16[128,1024]{1,0:T(8,128)(2,1)S(1)}, u32[]{:S(2)}, u32[]{:S(2)}) collective-permute-start(bf16[128,1024]{1,0:T(8,128)(2,1)S(1)} %slice.49), channel_id=1, source_target_pairs={{0,3},{1,0},{2,1},{3,2},{4,7},{5,4},{6,5},{7,6},{8,11},{9,8},{10,9... | collective-permute-start | bytes 786440 | tf_op jit(solution)/shard_map/ppermute | solution.py:347
  30.3 7.6 %collective-permute-done.5.rest_12_ = bf16[256,1024]{1,0:T(8,128)(2,1)S(1)} collective-permute-done((bf16[256,1024]{1,0:T(8,128)(2,1)S(1)}, bf16[256,1024]{1,0:T(8,128)(2,1)S(1)}, u32[]{:S(2)}, u32[]{:S(2)}) %collective-permute-start.5) | collective-permute-done | bytes 524320 | tf_op jit(solution)/shard_map/ppermute | solution.py:345
  37.9 3.5 %collective-permute-start.7 = (bf16[128,1024]{1,0:T(8,128)(2,1)S(1)}, bf16[128,1024]{1,0:T(8,128)(2,1)S(1)}, u32[]{:S(2)}, u32[]{:S(2)}) collective-permute-start(bf16[128,1024]{1,0:T(8,128)(2,1)S(1)} %slice.51), channel_id=1, source_target_pairs={{0,3},{1,0},{2,1},{3,2},{4,7},{5,4},{6,5},{7,6},{8,11},{9,8},{10,9... | collective-permute-start | bytes 786440 | tf_op jit(solution)/shard_map/ppermute | solution.py:347
  41.5 2.3 %lists.1 = (s32[1,256]{1,0:T(1,128)}, s32[1,256]{1,0:T(1,128)}) custom-call(s32[1,4]{1,0:T(1,128)} %counts.1, s32[4,2,240]{2,1,0:T(2,128)} %bitcast.22, s32[32,32]{1,0:T(8,128)} %bitcast.18), custom_call_target="tpu_custom_call" | custom-call | tf_op jit(solution)/shard_map/lists/pallas_call | solution.py:110
  43.9 2.8 %collective-permute-done.2.r2.rest_8_ = bf16[128,1024]{1,0:T(8,128)(2,1)S(1)} collective-permute-done((bf16[128,1024]{1,0:T(8,128)(2,1)S(1)}, bf16[128,1024]{1,0:T(8,128)(2,1)S(1)}, u32[]{:S(2)}, u32[]{:S(2)}) %collective-permute-start.2) | collective-permute-done | bytes 262176 | tf_op jit(solution)/shard_map/ppermute | solution.py:346
  46.6 0.7 copy-done.8
  47.3 15.4 %own.1 = (bf16[256,1024]{1,0:T(8,128)(2,1)}, bf16[256,1024]{1,0:T(8,128)(2,1)}, bf16[128,1024]{1,0:T(8,128)(2,1)}, bf16[128,1024]{1,0:T(8,128)(2,1)}, bf16[256,1024]{1,0:T(8,128)(2,1)}) custom-call(s32[1024]{0:T(1024)} %anchors.3, s32[32,32]{1,0:T(8,128)} %bitcast.19, s32[1,256]{1,0:T(1,128)} %get-tuple-element.25.listed, ...), custom_call_target="tpu_custom_call" | custom-call | tf_op jit(solution)/shard_map/own/pallas_call | solution.py:379
  62.7 0.7 copy-done.16
  63.4 0.1 copy-done.17
  63.5 18.0 %far.1 = (bf16[256,1024]{1,0:T(8,128)(2,1)}, bf16[256,1024]{1,0:T(8,128)(2,1)}, bf16[128,1024]{1,0:T(8,128)(2,1)}, bf16[128,1024]{1,0:T(8,128)(2,1)}, bf16[256,1...) custom-call(s32[1024]{0:T(1024)} %anchors.3, ...), custom_call_target="tpu_custom_call" | custom-call | tf_op jit(solution)/shard_map/far/pallas_call | solution.py:382
  81.6 0.5 collective-permute-start.14
  82.0 1.0 slice.41
  83.2 0.9 copy-done.12
  84.2 0.9 copy-done.18
  85.1 1.0 collective-permute-start.8
  86.1 1.6 %collective-permute-start.10 = (bf16[128,1024]{1,0:T(8,128)(2,1)S(1)}, bf16[128,1024]{1,0:T(8,128)(2,1)S(1)}, u32[]{:S(2)}, u32[]{:S(2)}) collective-permute-start(bf16[128,1024]{1,0:T(8,128)(2,1)S(1)} %copy-done.19), channel_id=1, source_target_pairs={{0,3},{1,0},{2,1},{3,2},{4,7},{5,4},{6,5},{7,6},{8,11},{9,8},{10,9... | collective-permute-start | bytes 786440 | tf_op jit(solution)/shard_map/ppermute | solution.py:356
  87.8 0.6 collective-permute-done.14
  88.5 2.2 %collective-permute-start.15 = (bf16[256,1024]{1,0:T(8,128)(2,1)S(1)}, bf16[256,1024]{1,0:T(8,128)(2,1)S(1)}, u32[]{:S(2)}, u32[]{:S(2)}) collective-permute-start(bf16[256,1024]{1,0:T(8,128)(2,1)S(1)} %pad_maximum_fusion.3), channel_id=1, source_target_pairs={{0,3},{1,0},{2,1},{3,2},{4,7},{5,4},{6,5},{7,6},{8,11},{9,8},{10,9... | collective-permute-start | bytes 1572872 | tf_op jit(solution)/shard_map/ppermute | solution.py:363
  90.6 7.9 %collective-permute-done.12 = bf16[128,1024]{1,0:T(8,128)(2,1)S(1)} collective-permute-done((bf16[128,1024]{1,0:T(8,128)(2,1)}, bf16[128,1024]{1,0:T(8,128)(2,1)S(1)}, u32[]{:S(2)}, u32[]{:S(2)}) %collective-permute-start.12) | collective-permute-done | bytes 262176 | tf_op jit(solution)/shard_map/ppermute | solution.py:355
  98.9 2.9 %collective-permute-start.11 = (bf16[256,1024]{1,0:T(8,128)(2,1)S(1)}, bf16[256,1024]{1,0:T(8,128)(2,1)S(1)}, u32[]{:S(2)}, u32[]{:S(2)}) collective-permute-start(bf16[256,1024]{1,0:T(8,128)(2,1)S(1)} %pad_maximum_fusion.1), channel_id=1, source_target_pairs={{0,3},{1,0},{2,1},{3,2},{4,7},{5,4},{6,5},{7,6},{8,11},{9,8},{10,9... | collective-permute-start | bytes 1572872 | tf_op jit(solution)/shard_map/ppermute | solution.py:363
  102.0 3.7 %collective-permute-done.15 = bf16[256,1024]{1,0:T(8,128)(2,1)S(1)} collective-permute-done((bf16[256,1024]{1,0:T(8,128)(2,1)S(1)}, bf16[256,1024]{1,0:T(8,128)(2,1)S(1)}, u32[]{:S(2)}, u32[]{:S(2)}) %collective-permute-start.15) | collective-permute-done | bytes 524320 | tf_op jit(solution)/shard_map/ppermute | solution.py:363
  105.7 5.6 %collective-permute-done.13 = bf16[256,1024]{1,0:T(8,128)(2,1)S(1)} collective-permute-done((bf16[256,1024]{1,0:T(8,128)(2,1)S(1)}, bf16[256,1024]{1,0:T(8,128)(2,1)S(1)}, u32[]{:S(2)}, u32[]{:S(2)}) %collective-permute-start.13) | collective-permute-done | bytes 524320 | tf_op jit(solution)/shard_map/ppermute | solution.py:363
  111.3 1.1 fusion
  112.4 12.3 %all-to-all-start.1 = ((bf16[32,8,1024]{2,1,0:T(8,128)(2,1)}), bf16[32,8,1024]{2,1,0:T(8,128)(2,1)S(1)}, u32[]{:S(2)}, u32[]{:S(2)}) async-start(bf16[32,8,1024]{2,1,0:T(8,128)(2,1)} %fusion), calls=%async_computation.1 | async-start | bytes 1048576 | tf_op jit(solution)/shard_map/all_to_all | solution.py:388
  124.7 11.4 %all-to-all-done.1 = bf16[32,8,1024]{2,1,0:T(8,128)(2,1)S(1)} async-done(((bf16[32,8,1024]{2,1,0:T(8,128)(2,1)}), bf16[32,8,1024]{2,1,0:T(8,128)(2,1)S(1)}, u32[]{:S(2)}, u32[]{:S(2)}) %all-to-all-start.1) | async-done | bytes 524320 | tf_op jit(solution)/shard_map/all_to_all | solution.py:388
  136.1 0.8 copy-done.4
  136.9 5.1 %finish.1 = f32[256,1024]{1,0:T(8,128)} custom-call(s32[32,32]{1,0:T(8,128)} %bitcast.21, bf16[256,1024]{1,0:T(8,128)(2,1)} %get-tuple-element.33.p0, bf16[256,1024]{1,0:T(8,128)(2,1)} %copy-done.15, bf16[256,1024]{1,0:T(8,128)(2,1)} %copy-done.14, bf16[256,1024]{1,0:T(8,128)(2,1)} %bitcast.14), custom_call_target="tpu_custom_call" | custom-call | tf_op jit(solution)/shard_map/finish/pallas_call | solution.py:389
  (66 shorter events, 1.0 us)
Async XLA Ops:
  3.3 9.6 %copy-start.3 = (bf16[256,1024]{1,0:T(8,128)(2,1)S(1)}, bf16[256,1024]{1,0:T(8,128)(2,1)}, u32[]{:S(2)}) copy-start(bf16[256,1024]{1,0:T(8,128)(2,1)} %get-tuple-element.26.s.rest_5_) | copy-start | bytes 1572868
  3.3 21.0 %all-to-all-start = ((bf16[32,8,1024]{2,1,0:T(8,128)(2,1)}), bf16[32,8,1024]{2,1,0:T(8,128)(2,1)S(1)}, u32[]{:S(2)}, u32[]{:S(2)}) async-start(bf16[32,8,1024]{2,1,0:T(8,128)(2,1)} %bitcast.16), calls=%async_computation | async-start | bytes 1048576 | tf_op jit(solution)/shard_map/all_to_all | solution.py:374
  12.8 14.2 %collective-permute-start.1 = (bf16[256,1024]{1,0:T(8,128)(2,1)S(1)}, bf16[256,1024]{1,0:T(8,128)(2,1)S(1)}, u32[]{:S(2)}, u32[]{:S(2)}) collective-permute-start(bf16[256,1024]{1,0:T(8,128)(2,1)S(1)} %copy-done.3), channel_id=1, source_target_pairs={{0,3},{1,0},{2,1},{3,2},{4,7},{5,4},{6,5},{7,6},{8,11},{9,8},{10,9... | collective-permute-start | bytes 1572872 | tf_op jit(solution)/shard_map/ppermute | solution.py:345
  15.6 14.6 %collective-permute-start = (bf16[256,1024]{1,0:T(8,128)(2,1)S(1)}, bf16[256,1024]{1,0:T(8,128)(2,1)S(1)}, u32[]{:S(2)}, u32[]{:S(2)}) collective-permute-start(bf16[256,1024]{1,0:T(8,128)(2,1)S(1)} %copy-done.3), channel_id=1, source_target_pairs={{0,1},{1,2},{2,3},{3,0},{4,5},{5,6},{6,7},{7,4},{8,9},{9,10},{10,1... | collective-permute-start | bytes 1572872 | tf_op jit(solution)/shard_map/ppermute | solution.py:344
  24.3 6.0 %copy-start.2 = (bf16[32,8,1024]{2,1,0:T(8,128)(2,1)}, bf16[32,8,1024]{2,1,0:T(8,128)(2,1)S(1)}, u32[]{:S(2)}) copy-start(bf16[32,8,1024]{2,1,0:T(8,128)(2,1)S(1)} %all-to-all-done) | copy-start | bytes 1572868
  24.3 13.6 %collective-permute-start.5 = (bf16[256,1024]{1,0:T(8,128)(2,1)S(1)}, bf16[256,1024]{1,0:T(8,128)(2,1)S(1)}, u32[]{:S(2)}, u32[]{:S(2)}) collective-permute-start(bf16[256,1024]{1,0:T(8,128)(2,1)S(1)} %bitcast.11), channel_id=1, source_target_pairs={{0,3},{1,0},{2,1},{3,2},{4,7},{5,4},{6,5},{7,6},{8,11},{9,8},{10,9... | collective-permute-start | bytes 1572872 | tf_op jit(solution)/shard_map/ppermute | solution.py:345
  27.0 14.4 %collective-permute-start.4 = (bf16[256,1024]{1,0:T(8,128)(2,1)S(1)}, bf16[256,1024]{1,0:T(8,128)(2,1)S(1)}, u32[]{:S(2)}, u32[]{:S(2)}) collective-permute-start(bf16[256,1024]{1,0:T(8,128)(2,1)S(1)} %bitcast.12), channel_id=1, source_target_pairs={{0,1},{1,2},{2,3},{3,0},{4,5},{5,6},{6,7},{7,4},{8,9},{9,10},{10,1... | collective-permute-start | bytes 1572872 | tf_op jit(solution)/shard_map/ppermute | solution.py:344
  27.0 10.9 %copy-start = (bf16[256,1024]{1,0:T(8,128)(2,1)}, bf16[256,1024]{1,0:T(8,128)(2,1)S(1)}, u32[]{:S(2)}) copy-start(bf16[256,1024]{1,0:T(8,128)(2,1)S(1)} %collective-permute-done.1.l.rest_7_) | copy-start | bytes 1572868
  27.0 16.8 %collective-permute-start.3 = (bf16[128,1024]{1,0:T(8,128)(2,1)S(1)}, bf16[128,1024]{1,0:T(8,128)(2,1)S(1)}, u32[]{:S(2)}, u32[]{:S(2)}) collective-permute-start(bf16[128,1024]{1,0:T(8,128)(2,1)S(1)} %slice.49), channel_id=1, source_target_pairs={{0,3},{1,0},{2,1},{3,2},{4,7},{5,4},{6,5},{7,6},{8,11},{9,8},{10,9... | collective-permute-start | bytes 786440 | tf_op jit(solution)/shard_map/ppermute | solution.py:347
  30.2 7.7 %copy-start.1 = (bf16[256,1024]{1,0:T(8,128)(2,1)}, bf16[256,1024]{1,0:T(8,128)(2,1)S(1)}, u32[]{:S(2)}) copy-start(bf16[256,1024]{1,0:T(8,128)(2,1)S(1)} %collective-permute-done.r.rest_6_) | copy-start | bytes 1572868
  30.2 16.4 %collective-permute-start.2 = (bf16[128,1024]{1,0:T(8,128)(2,1)S(1)}, bf16[128,1024]{1,0:T(8,128)(2,1)S(1)}, u32[]{:S(2)}, u32[]{:S(2)}) collective-permute-start(bf16[128,1024]{1,0:T(8,128)(2,1)S(1)} %slice.48), channel_id=1, source_target_pairs={{0,1},{1,2},{2,3},{3,0},{4,5},{5,6},{6,7},{7,4},{8,9},{9,10},{10,1... | collective-permute-start | bytes 786440 | tf_op jit(solution)/shard_map/ppermute | solution.py:346
  37.9 3.6 %copy-start.5 = (bf16[256,1024]{1,0:T(8,128)(2,1)}, bf16[256,1024]{1,0:T(8,128)(2,1)S(1)}, u32[]{:S(2)}) copy-start(bf16[256,1024]{1,0:T(8,128)(2,1)S(1)} %collective-permute-done.5.rest_12_) | copy-start | bytes 1572868
  37.9 24.8 %collective-permute-start.7 = (bf16[128,1024]{1,0:T(8,128)(2,1)S(1)}, bf16[128,1024]{1,0:T(8,128)(2,1)S(1)}, u32[]{:S(2)}, u32[]{:S(2)}) collective-permute-start(bf16[128,1024]{1,0:T(8,128)(2,1)S(1)} %slice.51), channel_id=1, source_target_pairs={{0,3},{1,0},{2,1},{3,2},{4,7},{5,4},{6,5},{7,6},{8,11},{9,8},{10,9... | collective-permute-start | bytes 786440 | tf_op jit(solution)/shard_map/ppermute | solution.py:347
  41.4 21.3 %copy-start.6 = (bf16[256,1024]{1,0:T(8,128)(2,1)}, bf16[256,1024]{1,0:T(8,128)(2,1)S(1)}, u32[]{:S(2)}) copy-start(bf16[256,1024]{1,0:T(8,128)(2,1)S(1)} %collective-permute-done.4.rest_11_) | copy-start | bytes 1572868
  41.4 21.3 %collective-permute-start.6 = (bf16[128,1024]{1,0:T(8,128)(2,1)S(1)}, bf16[128,1024]{1,0:T(8,128)(2,1)S(1)}, u32[]{:S(2)}, u32[]{:S(2)}) collective-permute-start(bf16[128,1024]{1,0:T(8,128)(2,1)S(1)} %slice.50), channel_id=1, source_target_pairs={{0,1},{1,2},{2,3},{3,0},{4,5},{5,6},{6,7},{7,4},{8,9},{9,10},{10,1... | collective-permute-start | bytes 786440 | tf_op jit(solution)/shard_map/ppermute | solution.py:346
  43.9 2.8 %copy-start.7 = (bf16[128,1024]{1,0:T(8,128)(2,1)}, bf16[128,1024]{1,0:T(8,128)(2,1)S(1)}, u32[]{:S(2)}) copy-start(bf16[128,1024]{1,0:T(8,128)(2,1)S(1)} %collective-permute-done.3.l2.rest_9_) | copy-start | bytes 786436
  81.5 1.5 %copy-start.10 = (bf16[256,1024]{1,0:T(8,128)(2,1)S(1)}, bf16[256,1024]{1,0:T(8,128)(2,1)}, u32[]{:S(2)}) copy-start(bf16[256,1024]{1,0:T(8,128)(2,1)} %get-tuple-element.36) | copy-start | bytes 1572868
  81.6 6.8 %collective-permute-start.14 = (bf16[128,1024]{1,0:T(8,128)(2,1)}, bf16[128,1024]{1,0:T(8,128)(2,1)S(1)}, u32[]{:S(2)}, u32[]{:S(2)}) collective-permute-start(bf16[128,1024]{1,0:T(8,128)(2,1)} %get-tuple-element.42), channel_id=1, source_target_pairs={{0,3},{1,0},{2,1},{3,2},{4,7},{5,4},{6,5},{7,6},{8,11},{9,8},{10,9... | collective-permute-start | bytes 786440 | tf_op jit(solution)/shard_map/ppermute | solution.py:356
  82.0 1.2 copy-start.11
  84.1 2.0 %copy-start.19 = (bf16[128,1024]{1,0:T(8,128)(2,1)S(1)}, bf16[128,1024]{1,0:T(8,128)(2,1)}, u32[]{:S(2)}) copy-start(bf16[128,1024]{1,0:T(8,128)(2,1)} %get-tuple-element.37) | copy-start | bytes 786436
  85.1 16.7 %collective-permute-start.8 = (bf16[128,1024]{1,0:T(8,128)(2,1)S(1)}, bf16[128,1024]{1,0:T(8,128)(2,1)S(1)}, u32[]{:S(2)}, u32[]{:S(2)}) collective-permute-start(bf16[128,1024]{1,0:T(8,128)(2,1)S(1)} %copy-done.18), channel_id=1, source_target_pairs={{0,1},{1,2},{2,3},{3,0},{4,5},{5,6},{6,7},{7,4},{8,9},{9,10},{10,1... | collective-permute-start | bytes 786440 | tf_op jit(solution)/shard_map/ppermute | solution.py:355
  86.1 12.6 %collective-permute-start.10 = (bf16[128,1024]{1,0:T(8,128)(2,1)S(1)}, bf16[128,1024]{1,0:T(8,128)(2,1)S(1)}, u32[]{:S(2)}, u32[]{:S(2)}) collective-permute-start(bf16[128,1024]{1,0:T(8,128)(2,1)S(1)} %copy-done.19), channel_id=1, source_target_pairs={{0,3},{1,0},{2,1},{3,2},{4,7},{5,4},{6,5},{7,6},{8,11},{9,8},{10,9... | collective-permute-start | bytes 786440 | tf_op jit(solution)/shard_map/ppermute | solution.py:356
  87.8 10.8 %collective-permute-start.12 = (bf16[128,1024]{1,0:T(8,128)(2,1)}, bf16[128,1024]{1,0:T(8,128)(2,1)S(1)}, u32[]{:S(2)}, u32[]{:S(2)}) collective-permute-start(bf16[128,1024]{1,0:T(8,128)(2,1)} %get-tuple-element.40), channel_id=1, source_target_pairs={{0,1},{1,2},{2,3},{3,0},{4,5},{5,6},{6,7},{7,4},{8,9},{9,10},{10,1... | collective-permute-start | bytes 786440 | tf_op jit(solution)/shard_map/ppermute | solution.py:355
  88.5 17.2 %collective-permute-start.15 = (bf16[256,1024]{1,0:T(8,128)(2,1)S(1)}, bf16[256,1024]{1,0:T(8,128)(2,1)S(1)}, u32[]{:S(2)}, u32[]{:S(2)}) collective-permute-start(bf16[256,1024]{1,0:T(8,128)(2,1)S(1)} %pad_maximum_fusion.3), channel_id=1, source_target_pairs={{0,3},{1,0},{2,1},{3,2},{4,7},{5,4},{6,5},{7,6},{8,11},{9,8},{10,9... | collective-permute-start | bytes 1572872 | tf_op jit(solution)/shard_map/ppermute | solution.py:363
  98.6 12.7 %collective-permute-start.13 = (bf16[256,1024]{1,0:T(8,128)(2,1)S(1)}, bf16[256,1024]{1,0:T(8,128)(2,1)S(1)}, u32[]{:S(2)}, u32[]{:S(2)}) collective-permute-start(bf16[256,1024]{1,0:T(8,128)(2,1)S(1)} %pad_maximum_fusion.2), channel_id=1, source_target_pairs={{0,1},{1,2},{2,3},{3,0},{4,5},{5,6},{6,7},{7,4},{8,9},{9,10},{10,1... | collective-permute-start | bytes 1572872 | tf_op jit(solution)/shard_map/ppermute | solution.py:363
  98.8 3.0 %copy-start.9 = (bf16[256,1024]{1,0:T(8,128)(2,1)S(1)}, bf16[256,1024]{1,0:T(8,128)(2,1)}, u32[]{:S(2)}) copy-start(bf16[256,1024]{1,0:T(8,128)(2,1)} %get-tuple-element.34) | copy-start | bytes 1572868
  98.9 25.8 %collective-permute-start.11 = (bf16[256,1024]{1,0:T(8,128)(2,1)S(1)}, bf16[256,1024]{1,0:T(8,128)(2,1)S(1)}, u32[]{:S(2)}, u32[]{:S(2)}) collective-permute-start(bf16[256,1024]{1,0:T(8,128)(2,1)S(1)} %pad_maximum_fusion.1), channel_id=1, source_target_pairs={{0,3},{1,0},{2,1},{3,2},{4,7},{5,4},{6,5},{7,6},{8,11},{9,8},{10,9... | collective-permute-start | bytes 1572872 | tf_op jit(solution)/shard_map/ppermute | solution.py:363
  101.8 9.5 %copy-start.13 = (bf16[256,1024]{1,0:T(8,128)(2,1)S(1)}, bf16[256,1024]{1,0:T(8,128)(2,1)}, u32[]{:S(2)}) copy-start(bf16[256,1024]{1,0:T(8,128)(2,1)} %get-tuple-element.38) | copy-start | bytes 1572868
  101.9 22.8 %collective-permute-start.9 = (bf16[256,1024]{1,0:T(8,128)(2,1)S(1)}, bf16[256,1024]{1,0:T(8,128)(2,1)S(1)}, u32[]{:S(2)}, u32[]{:S(2)}) collective-permute-start(bf16[256,1024]{1,0:T(8,128)(2,1)S(1)} %pad_maximum_fusion), channel_id=1, source_target_pairs={{0,1},{1,2},{2,3},{3,0},{4,5},{5,6},{6,7},{7,4},{8,9},{9,10},{10,1... | collective-permute-start | bytes 1572872 | tf_op jit(solution)/shard_map/ppermute | solution.py:363
  112.4 23.7 %all-to-all-start.1 = ((bf16[32,8,1024]{2,1,0:T(8,128)(2,1)}), bf16[32,8,1024]{2,1,0:T(8,128)(2,1)S(1)}, u32[]{:S(2)}, u32[]{:S(2)}) async-start(bf16[32,8,1024]{2,1,0:T(8,128)(2,1)} %fusion), calls=%async_computation.1 | async-start | bytes 1048576 | tf_op jit(solution)/shard_map/all_to_all | solution.py:388
  124.7 11.4 %copy-start.14 = (bf16[256,1024]{1,0:T(8,128)(2,1)}, bf16[256,1024]{1,0:T(8,128)(2,1)S(1)}, u32[]{:S(2)}) copy-start(bf16[256,1024]{1,0:T(8,128)(2,1)S(1)} %collective-permute-done.11.p2) | copy-start | bytes 1572868
  124.7 11.4 %copy-start.15 = (bf16[256,1024]{1,0:T(8,128)(2,1)}, bf16[256,1024]{1,0:T(8,128)(2,1)S(1)}, u32[]{:S(2)}) copy-start(bf16[256,1024]{1,0:T(8,128)(2,1)S(1)} %collective-permute-done.9.p1) | copy-start | bytes 1572868
  (6 other events, 5.0 us)
